TPU v7x, 32 devices: a whole 2x2x4 slice. The times are simulated.
32 devices in a mesh: dom: 32 (over z, y, x, core).
Axes of the slice: x: 2, y: 2, z: 4, core: 2. Of those that a mesh axis runs over, the one named last changes fastest.
Arguments:
- rest_pos: float32 [3, 131072], P(None, 'dom'), may hold values from -6 to 6
- displacement: float32 [3, 131072], P(None, 'dom'), may hold values from -3 to 3
- velocity: float32 [3, 131072], P(None, 'dom'), may hold values from -6 to 6
- ext_force: float32 [3, 131072], P(None, 'dom'), may hold values from -6 to 6
- node_mass: float32 [131072], P('dom'), may hold values from 0.5 to 2
- body_accel: float32 [3], replicated, may hold values from -2 to 2
- connectivity: int32 [8, 131072], P(None, 'dom'), may hold values from 0 to 4095
- elem_material: int32 [1024], P('dom'), may hold values from 0 to 7
- stiffness: float32 [8, 24, 24], replicated, may hold values from -1.25 to 1.25
- shared_nodes: int32 [32, 5, 128], P('dom'), may hold values from 0 to 4095, as said below
- contact_slave: int32 [65536], P('dom'), may hold values from 0 to 4095
- contact_owner: int32 [65536, 1], P('dom'), may hold values from 0 to 31; in each aligned block of 2048 rows (0 to 2047, 2048 to 4095, ...) at most 256 rows name the same one
- contact_master: int32 [65536], P('dom'), may hold values from 0 to 4095
- contact_normal: float32 [3, 65536], P(None, 'dom'), may hold values from -4 to 4
- part_of_node: int32 [131072], P('dom'), may hold values from 0 to 799
- part_mass: float32 [400], replicated, may hold values from 81 to 327
- part_center: float32 [3, 400], replicated, may hold values from -1 to 1
- part_inertia: float32 [3, 400], replicated, may hold values from 81 to 327
Outputs:
- nodal_velocity: float32 [3, 131072], P(None, 'dom')
- part_motion: float32 [6, 400], replicated
Inputs may be any that keep to these rules, and one draw needn't show every extreme that they name: `connectivity`: offsets are taken modulo 4096 after adding the element's own local number. `shared_nodes`: on each partition d the 5 x 128 entries are distinct interface copies; entry k of list b on d and entry k of list b on d XOR 2**b are copies of one node. `contact_slave`: slave indices are local copies of the contact's own partition. `contact_owner`: among the 2048 contacts of one partition no owner appears more than 256 times, and some owner appears exactly 256 times. `contact_master`: master indices are local copies of the owner partition. `part_of_node`: values of 400 or more mark copies of no rigid part.
All inputs are finite; a program needn't handle non-finite values.
Results may differ from a plain program's by a relative error of at most 0.0001.
Values sent between devices are 32-bit elements; how exact they have to be, the bound alone decides.
A program may use at most 128 MiB of HBM per device.

v0:
```python
import jax
import jax.numpy as jnp
from jax import lax
from jax.sharding import PartitionSpec as P

CYCLES = 3
PARTS_SIZE = 400


TIME_STEP = 0.1
DAMP_RATIO = 0.05
PENALTY = 2.0
GAP_WIDTH = 0.5
CONTACT_DAMP = 0.2


def partner(block, axis, apart):
    count = lax.axis_size(axis)
    route = []
    for low in range(count):
        high = low | 1 << apart
        if high != low and high < count:
            route += [(low, high), (high, low)]
    return lax.ppermute(block, axis, route)


def element_forces(corners, material, stiffness, nodal_field):
    blocks = corners.shape[1] // 128
    material_count = stiffness.shape[0]
    onehot = (material[:, None] == jnp.arange(material_count, dtype=jnp.int32)[None, :]).astype(
        jnp.float32
    )
    block_matrix = jnp.dot(
        onehot, stiffness.reshape(material_count, 576), precision=lax.Precision.HIGHEST
    ).reshape(blocks, 24, 24)
    gathered = nodal_field[:, corners].reshape(24, blocks, 128)
    forces = jnp.einsum("bij,jbk->ibk", block_matrix, gathered, precision=lax.Precision.HIGHEST)
    return (
        jnp.zeros_like(nodal_field)
        .at[:, corners.reshape(-1)]
        .add(forces.reshape(3, 8 * corners.shape[1]))
    )


def contact_push(slave_pos, slave_vel, master_pos, master_vel, normal):
    gap_size = jnp.sum((slave_pos - master_pos) * normal, axis=0)
    closing = jnp.sum((slave_vel - master_vel) * normal, axis=0)
    push_size = (
        PENALTY * GAP_WIDTH * jax.nn.softplus(-gap_size / GAP_WIDTH) - CONTACT_DAMP * closing
    )
    return push_size[None] * normal


def cross_product(left, right):
    return jnp.stack(
        [
            left[1] * right[2] - left[2] * right[1],
            left[2] * right[0] - left[0] * right[2],
            left[0] * right[1] - left[1] * right[0],
        ]
    )


def per_device(
    rest_pos,
    displacement,
    velocity,
    ext_force,
    node_mass,
    body_accel,
    connectivity,
    elem_material,
    stiffness,
    shared_nodes,
    contact_slave,
    contact_owner,
    contact_master,
    contact_normal,
    part_of_node,
    part_mass,
    part_center,
    part_inertia,
):
    domains = lax.axis_size("dom")
    neighbours = shared_nodes.shape[1]
    shared_count = shared_nodes.shape[2]
    shared_flat = shared_nodes.reshape(-1)
    accel_column = body_accel[:, None]
    node_count = displacement.shape[1]
    local_elem = jnp.arange(connectivity.shape[1], dtype=jnp.int32)
    corners = (connectivity + local_elem[None, :]) % node_count
    displaced = displacement
    speeds = velocity
    assembled = jnp.zeros_like(displacement)
    for cycle_index in range(CYCLES):
        internal = element_forces(
            corners, elem_material, stiffness, displaced + DAMP_RATIO * speeds
        )
        own_values = internal[:, shared_flat].reshape(3, neighbours, shared_count)
        received = []
        for bit_number in range(neighbours):
            received.append(partner(own_values[:, bit_number], "dom", bit_number))
        assembled = internal.at[:, shared_flat].add(
            jnp.stack(received, axis=1).reshape(3, neighbours * shared_count)
        )
        speeds = speeds + TIME_STEP * ((ext_force - assembled) / node_mass[None] - accel_column)
        displaced = displaced + TIME_STEP * speeds
    positions = rest_pos + displaced
    contacts = contact_slave.shape[0]
    capacity = 4 * contacts // domains
    owners = contact_owner[:, 0]
    owner_hits = (owners[:, None] == jnp.arange(domains, dtype=jnp.int32)[None, :]).astype(
        jnp.int32
    )
    slot_rank = jnp.sum(jnp.cumsum(owner_hits, axis=0) * owner_hits, axis=1) - 1
    slot_index = owners * capacity + slot_rank
    slave_pos = positions[:, contact_slave]
    slave_vel = speeds[:, contact_slave]
    contact_force = jnp.zeros_like(positions)
    payload = jnp.zeros((10, domains * capacity), jnp.float32).at[9].set(-1.0)
    payload = payload.at[:, slot_index].set(
        jnp.concatenate(
            [slave_pos, slave_vel, contact_normal, contact_master[None].astype(jnp.float32)], 0
        )
    )
    payload = payload.reshape(10, domains, capacity)
    arrived = lax.all_to_all(payload, "dom", split_axis=1, concat_axis=1, tiled=True)
    valid_slot = (arrived[9] >= 0.0).astype(jnp.float32)
    master_index = jnp.maximum(arrived[9], 0.0).astype(jnp.int32)
    pushed = (
        contact_push(
            arrived[0:3],
            arrived[3:6],
            positions[:, master_index],
            speeds[:, master_index],
            arrived[6:9],
        )
        * valid_slot[None]
    )
    returned = lax.all_to_all(pushed, "dom", split_axis=1, concat_axis=1, tiled=True)
    returned, pushed, master_float = (returned, pushed, arrived[9:10])
    master_index = jnp.maximum(master_float, 0.0).astype(jnp.int32)
    contact_force = contact_force.at[:, master_index.reshape(-1)].add(-pushed.reshape(3, -1))
    slave_push = returned.reshape(3, domains * capacity)[:, slot_index]
    contact_force = contact_force.at[:, contact_slave].add(slave_push)
    nodal_velocity = speeds + TIME_STEP * contact_force / node_mass[None]
    net_force = ext_force - assembled + contact_force - node_mass[None] * accel_column
    part_index = jnp.minimum(part_of_node, PARTS_SIZE)
    weighted = jnp.concatenate([node_mass[None], node_mass[None] * positions], 0)
    totals = lax.psum(
        jax.ops.segment_sum(
            jnp.concatenate([weighted, net_force, cross_product(positions, net_force)], 0).T,
            part_index,
            PARTS_SIZE + 1,
        )[:PARTS_SIZE].T,
        "dom",
    )
    mass_total = part_mass + totals[0]
    centre = (part_mass[None] * part_center + totals[1:4]) / mass_total[None]
    force_sum = totals[4:7]
    torque = totals[7:10] - cross_product(centre, force_sum)
    part_motion = jnp.concatenate([force_sum / mass_total[None], torque / part_inertia], 0)
    return (nodal_velocity, part_motion)


def solution(mesh):
    placed = (
        P(None, "dom"),
        P(None, "dom"),
        P(None, "dom"),
        P(None, "dom"),
        P("dom"),
        P(),
        P(None, "dom"),
        P("dom"),
        P(),
        P("dom", None, None),
        P("dom"),
        P("dom", None),
        P("dom"),
        P(None, "dom"),
        P("dom"),
        P(),
        P(),
        P(),
    )
    return jax.shard_map(
        per_device, mesh=mesh, in_specs=placed, out_specs=(P(None, "dom"), P()), check_vma=False
    )
```

profile of v0, /device:TPU:0, one launch (start us, length us, event | category | flops | bytes accessed | tf_op | source)
XLA Modules:
  0.0 1264.4 jit_solution(16717740665865341079)
XLA Ops:
  5.1 109.0 %gather_fusion = f32[32768,3]{1,0:T(8,128)} fusion(f32[3,4096]{0,1:T(8,128)S(1)} %copy.282, s32[32768]{0:T(1024)S(1)} %broadcast_clamp_fusion), kind=kCustom, calls=%fused_computation | custom fusion | bytes 917504 | tf_op jit(solution)/shard_map/gather | solution.py:36
  114.1 9.8 copy.283
  125.3 8.6 copy.288
  133.9 174.7 %scatter_custom_fusion = f32[3,4096]{0,1:T(8,128)S(1)} fusion(s32[32768]{0:T(1024)S(1)} %bitcast.187, f32[32768,3]{1,0:T(8,128)} %copy.288, f32[]{:T(128)} %constant.76.clone.1), kind=kCustom, calls=%fused_computation.32 | custom fusion | flops 98304 | bytes 49664 | tf_op jit(solution)/shard_map/scatter-add | solution.py:41
  320.1 9.1 reduce-window.6
  333.0 7.4 scatter_fusion
  342.4 109.0 %gather_fusion.2 = f32[32768,3]{1,0:T(8,128)} fusion(f32[3,4096]{0,1:T(8,128)S(1)} %copy.296, s32[32768]{0:T(1024)S(1)} %broadcast_clamp_fusion), kind=kCustom, calls=%fused_computation.2 | custom fusion | bytes 917504 | tf_op jit(solution)/shard_map/gather | solution.py:36
  451.4 9.8 copy.297
  462.5 8.6 copy.301
  471.1 174.7 %scatter_custom_fusion.2 = f32[3,4096]{0,1:T(8,128)S(1)} fusion(s32[32768]{0:T(1024)S(1)} %bitcast.188, f32[32768,3]{1,0:T(8,128)} %copy.301, f32[]{:T(128)} %constant.76.clone.1), kind=kCustom, calls=%fused_computation.30 | custom fusion | flops 98304 | bytes 49664 | tf_op jit(solution)/shard_map/scatter-add | solution.py:41
  657.1 7.4 scatter_fusion.1
  665.9 109.0 %gather_fusion.4 = f32[32768,3]{1,0:T(8,128)} fusion(f32[3,4096]{0,1:T(8,128)S(1)} %copy.309, s32[32768]{0:T(1024)S(1)} %broadcast_clamp_fusion), kind=kCustom, calls=%fused_computation.4 | custom fusion | bytes 917504 | tf_op jit(solution)/shard_map/gather | solution.py:36
  774.9 9.8 copy.310
  786.0 8.6 copy.314
  794.6 174.7 %scatter_custom_fusion.4 = f32[3,4096]{0,1:T(8,128)S(1)} fusion(s32[32768]{0:T(1024)S(1)} %bitcast.189, f32[32768,3]{1,0:T(8,128)} %copy.314, f32[]{:T(128)} %constant.76.clone.1), kind=kCustom, calls=%fused_computation.28 | custom fusion | flops 98304 | bytes 49664 | tf_op jit(solution)/shard_map/scatter-add | solution.py:41
  971.8 4.4 copy.400
  986.4 7.1 scatter_fusion.2
  994.9 6.6 gather_fusion.7
  1004.4 7.0 gather_fusion.6
  1013.6 9.8 scatter_fusion.3
  1023.4 3.6 copy.329
  1029.6 15.6 %all-to-all-done = f32[10,32,256]{2,0,1:T(8,128)S(1)} async-done(((f32[10,32,256]{2,0,1:T(8,128)}), f32[10,32,256]{2,0,1:T(8,128)S(1)}, u32[]{:S(2)}, u32[]{:S(2)}) %all-to-all-start) | async-done | bytes 327712 | tf_op jit(solution)/shard_map/all_to_all | solution.py:127
  1045.3 29.5 %gather_fusion.8 = f32[8192,3]{1,0:T(8,128)} fusion(f32[3,4096]{0,1:T(8,128)} %copy.324, s32[8192]{0:T(1024)S(1)} %broadcast_clamp_fusion.1), kind=kCustom, calls=%fused_computation.8 | custom fusion | bytes 229376 | tf_op jit(solution)/shard_map/gather | solution.py:134
  1074.8 27.9 %gather_fusion.9 = f32[8192,3]{1,0:T(8,128)} fusion(f32[3,4096]{0,1:T(8,128)S(1)} %copy.325, s32[8192]{0:T(1024)S(1)} %broadcast_clamp_fusion.1), kind=kCustom, calls=%fused_computation.9 | custom fusion | bytes 229376 | tf_op jit(solution)/shard_map/gather | solution.py:135
  1102.8 2.8 copy.332
  1105.6 2.9 copy.334
  1109.5 2.9 all-to-all-start.1
  1112.4 2.6 copy.335
  1115.0 45.7 %scatter_custom_fusion.7 = f32[3,4096]{0,1:T(8,128)S(1)} fusion(s32[8192]{0:T(1024)S(1)} %bitcast.201, f32[8192,3]{1,0:T(8,128)} %copy.335, f32[]{:T(128)} %constant.76.clone.1), kind=kCustom, calls=%fused_computation.26 | custom fusion | flops 24576 | bytes 49664 | tf_op jit(solution)/shard_map/scatter-add | solution.py:143
  1163.4 24.1 %scatter_custom_fusion.8 = f32[3,4096]{0,1:T(8,128)S(1)} fusion(f32[3,4096]{0,1:T(8,128)S(1)} %scatter_custom_fusion.7, s32[2048]{0:T(1024)} %get-tuple-element.61, f32[3,8192]{0,1:T(8,128)} %bitcast.166, s32[2048]{0:T(1024)S(1)} %broadcast_clamp_fusion.2), kind=kCustom, calls=%fused_computation.24 | custom fusion | flops 6144 | bytes 49152 | tf_op jit(solution)/shard_map/scatter-add | solution.py:145
  1189.7 22.4 %scatter_custom_fusion.9 = f32[401,10]{1,0:T(8,128)S(1)} fusion(s32[4096]{0:T(1024)S(1)} %broadcast_minimum_fusion, f32[4096,10]{1,0:T(8,128)S(1)} %copy.339, f32[]{:T(128)} %constant.76.clone.1), kind=kCustom, calls=%fused_computation.60 | custom fusion | flops 40960 | bytes 16044 | tf_op jit(solution)/shard_map/scatter-add | solution.py:151
  1212.3 50.9 %psum.7 = f32[10,400]{1,0:T(8,128)S(1)} all-reduce(f32[10,400]{1,0:T(8,128)S(1)} %bitcast.192), channel_id=1, replica_groups=mesh['dom'=32] {'dom'}, use_global_device_ids=true, to_apply=%region_15.16 | all-reduce | flops 4000 | bytes 32000 | tf_op jit(solution)/shard_map/psum | solution.py:150
  (197 shorter events, 66.5 us)
Async XLA Ops:
  133.8 186.2 %copy-start.9 = (s32[2048,1]{0,1:T(1,128)S(1)}, s32[2048,1]{0,1:T(1,128)}, u32[]{:S(2)}) copy-start(s32[2048,1]{0,1:T(1,128)} %param.31) | copy-start | bytes 24580
  133.9 176.5 %copy-start.4 = (s32[640]{0:T(1024)}, s32[640]{0:T(1024)S(1)}, u32[]{:S(2)}) copy-start(s32[640]{0:T(1024)S(1)} %fusion.33) | copy-start | bytes 7684
  133.9 186.2 %copy-start.13 = (s32[1024]{0:T(1024)}, s32[1024]{0:T(1024)S(1)}, u32[]{:S(2)}) copy-start(s32[1024]{0:T(1024)S(1)} %pad_clamp_fusion) | copy-start | bytes 12292
  311.0 21.9 %copy-start.5 = (s32[640]{0:T(1024)S(1)}, s32[640]{0:T(1024)}, u32[]{:S(2)}) copy-start(s32[640]{0:T(1024)} %copy-done.4) | copy-start | bytes 7684
  311.0 19.6 %collective-permute-start = (f32[3,128]{1,0:T(4,128)}, f32[3,128]{1,0:T(4,128)}, u32[]{:S(2)}, u32[]{:S(2)}) collective-permute-start(f32[3,128]{1,0:T(4,128)} %bitcast.10), channel_id=1, source_target_pairs={{0,1},{1,0},{2,3},{3,2},{4,5},{5,4},{6,7},{7,6},{8,9},{9,8},{10,11... | collective-permute-start | bytes 4616 | tf_op jit(solution)/shard_map/ppermute | solution.py:24
  311.6 19.8 %collective-permute-start.1 = (f32[3,128]{1,0:T(4,128)S(1)}, f32[3,128]{1,0:T(4,128)}, u32[]{:S(2)}, u32[]{:S(2)}) collective-permute-start(f32[3,128]{1,0:T(4,128)S(1)} %bitcast.210), channel_id=1, source_target_pairs={{0,2},{2,0},{1,3},{3,1},{4,6},{6,4},{5,7},{7,5},{8,10},{10,8},{9,1... | collective-permute-start | bytes 4616 | tf_op jit(solution)/shard_map/ppermute | solution.py:24
  314.1 17.9 %collective-permute-start.2 = (f32[3,128]{1,0:T(4,128)S(1)}, f32[3,128]{1,0:T(4,128)S(1)}, u32[]{:S(2)}, u32[]{:S(2)}) collective-permute-start(f32[3,128]{1,0:T(4,128)S(1)} %bitcast.209), channel_id=1, source_target_pairs={{0,4},{4,0},{1,5},{5,1},{2,6},{6,2},{3,7},{7,3},{8,12},{12,8},{9,1... | collective-permute-start | bytes 4616 | tf_op jit(solution)/shard_map/ppermute | solution.py:24
  315.8 16.3 %collective-permute-start.3 = (f32[3,128]{1,0:T(4,128)S(1)}, f32[3,128]{1,0:T(4,128)S(1)}, u32[]{:S(2)}, u32[]{:S(2)}) collective-permute-start(f32[3,128]{1,0:T(4,128)S(1)} %bitcast.207), channel_id=1, source_target_pairs={{0,8},{8,0},{1,9},{9,1},{2,10},{10,2},{3,11},{11,3},{4,12},{12,4},... | collective-permute-start | bytes 4616 | tf_op jit(solution)/shard_map/ppermute | solution.py:24
  317.4 14.6 %collective-permute-start.4 = (f32[3,128]{1,0:T(4,128)S(1)}, f32[3,128]{1,0:T(4,128)S(1)}, u32[]{:S(2)}, u32[]{:S(2)}) collective-permute-start(f32[3,128]{1,0:T(4,128)S(1)} %bitcast.208), channel_id=1, source_target_pairs={{0,16},{16,0},{1,17},{17,1},{2,18},{18,2},{3,19},{19,3},{4,20},{20... | collective-permute-start | bytes 4616 | tf_op jit(solution)/shard_map/ppermute | solution.py:24
  471.1 174.8 %copy-start.14 = (s32[1024]{0:T(1024)S(1)}, s32[1024]{0:T(1024)}, u32[]{:S(2)}) copy-start(s32[1024]{0:T(1024)} %copy-done.13) | copy-start | bytes 12292
  471.1 178.1 %copy-start.10 = (s32[2048,1]{0,1:T(1,128)S(1)}, s32[2048,1]{0,1:T(1,128)}, u32[]{:S(2)}) copy-start(s32[2048,1]{0,1:T(1,128)} %param.31) | copy-start | bytes 24580
  471.1 186.0 %copy-start.6 = (s32[640]{0:T(1024)S(1)}, s32[640]{0:T(1024)}, u32[]{:S(2)}) copy-start(s32[640]{0:T(1024)} %copy-done.4) | copy-start | bytes 7684
  645.9 19.3 %copy-start.16 = (f32[3]{0:T(128)S(1)}, f32[3]{0:T(128)}, u32[]{:S(2)}) copy-start(f32[3]{0:T(128)} %param.25) | copy-start | bytes 40
  649.2 2.5 collective-permute-start.5
  649.9 3.6 collective-permute-start.6
  650.5 3.6 collective-permute-start.7
  651.1 3.6 collective-permute-start.8
  651.7 4.5 collective-permute-start.9
  794.6 176.6 %copy-start.19 = (s32[2048]{0:T(1024)S(1)}, s32[2048]{0:T(1024)}, u32[]{:S(2)}) copy-start(s32[2048]{0:T(1024)} %param.30) | copy-start | bytes 24580
  971.1 10.9 collective-permute-start.10
  976.2 17.9 %copy-start.12 = (f32[3,4096]{1,0:T(4,128)S(1)}, f32[3,4096]{1,0:T(4,128)}, u32[]{:S(2)}) copy-start(f32[3,4096]{1,0:T(4,128)} %param.20) | copy-start | bytes 147460
  976.2 17.9 %copy-start.17 = (f32[3]{0:T(128)S(1)}, f32[3]{0:T(128)}, u32[]{:S(2)}) copy-start(f32[3]{0:T(128)} %param.25) | copy-start | bytes 40
  976.9 5.2 collective-permute-start.11
  978.4 3.7 collective-permute-start.12
  980.0 3.6 collective-permute-start.13
  981.7 4.5 collective-permute-start.14
  1027.0 18.2 %all-to-all-start = ((f32[10,32,256]{2,0,1:T(8,128)}), f32[10,32,256]{2,0,1:T(8,128)S(1)}, u32[]{:S(2)}, u32[]{:S(2)}) async-start(f32[10,32,256]{2,0,1:T(8,128)} %copy.329), calls=%async_computation | async-start | bytes 1048576 | tf_op jit(solution)/shard_map/all_to_all | solution.py:127
  1109.5 51.3 %all-to-all-start.1 = ((f32[3,32,256]{2,0,1:T(4,128)}), f32[3,32,256]{2,0,1:T(4,128)S(1)}, u32[]{:S(2)}, u32[]{:S(2)}) async-start(f32[3,32,256]{2,0,1:T(4,128)} %get-tuple-element.29), calls=%async_computation.1 | async-start | bytes 262144 | tf_op jit(solution)/shard_map/all_to_all | solution.py:140
  1163.4 24.8 %copy-start.18 = (f32[3]{0:T(128)S(1)}, f32[3]{0:T(128)}, u32[]{:S(2)}) copy-start(f32[3]{0:T(128)} %param.25) | copy-start | bytes 40
  1188.2 75.0 %copy-start.20 = (f32[400]{0:T(512)S(1)}, f32[400]{0:T(512)}, u32[]{:S(2)}) copy-start(f32[400]{0:T(512)} %param.35) | copy-start | bytes 4804
  1188.2 75.1 %copy-start.22 = (f32[3,400]{1,0:T(4,128)S(1)}, f32[3,400]{1,0:T(4,128)}, u32[]{:S(2)}) copy-start(f32[3,400]{1,0:T(4,128)} %param.36) | copy-start | bytes 14404
  1188.2 75.1 %copy-start.23 = (f32[3,400]{1,0:T(4,128)S(1)}, f32[3,400]{1,0:T(4,128)}, u32[]{:S(2)}) copy-start(f32[3,400]{1,0:T(4,128)} %param.37) | copy-start | bytes 14404
  (10 other events, 80.7 us)
where the time goes:
time: 1270 us; the launch traced here: 1260 us
  other arithmetic  656 us (52%)
  local copies, waits for them, and re-layouts  507 us (40%)
  blocking collectives  50.9 us (4%)
  waiting for transfers between devices  24.1 us (2%)
  starting transfers between devices  21 us (2%)
    scatter-add x3, other arithmetic, element_forces(): return jnp.zeros_like(nodal_field).at[:, corners.reshape(-1)].add(forces....  524 us
    gather x6, local copies, waits for them, and re-layouts, element_forces(): gathered = nodal_field[:, corners].reshape(24, blocks, 128)  356 us
    psum x1, blocking collectives, per_device(): lax.psum(jax.ops.segment_sum(jnp.concatenate([weighted, net_force, cross_...  50.9 us
    scatter-add x1, other arithmetic, per_device(): contact_force.at[:, master_index.reshape(-1)].add(-pushed.reshape(3, -1))  45.7 us
    gather x2, local copies, waits for them, and re-layouts, per_device(): positions[:, master_index]  32.3 us
    gather x2, local copies, waits for them, and re-layouts, per_device(): speeds[:, master_index]  30.8 us
    reshape x6, local copies, waits for them, and re-layouts, element_forces(): forces.reshape(3, 8 * corners.shape[1])  26.3 us
  transfers between devices with their start and end apart: 17, of which 7 were waited for; matrix products, arithmetic and copies ran while one was open for 5% of the time, Pallas kernels for 0%

commit v1 on v0

v1 whole, which is shorter than its diff:
```python
import functools

import jax
import jax.numpy as jnp
from jax import lax
from jax.experimental import pallas as pl
from jax.experimental.pallas import tpu as pltpu
from jax.sharding import PartitionSpec as P

CYCLES = 3
PARTS_SIZE = 400
TIME_STEP = 0.1
DAMP_RATIO = 0.05
PENALTY = 2.0
GAP_WIDTH = 0.5
CONTACT_DAMP = 0.2
L = 128
F32 = jnp.float32
BF16 = jnp.bfloat16
NT = (((1,), (1,)), ((), ()))


def split_pieces(value, pieces):
    out = []
    for _ in range(pieces):
        piece = value.astype(BF16)
        out.append(piece)
        value = value - piece.astype(F32)
    return out


def row_of(value, row, count):
    return jnp.broadcast_to(value[row : row + 1, :], (count, L))


def lookup(tables, index):
    high = index >> 7
    low = index & 127
    found = [None] * len(tables[0])
    for r, rows in enumerate(tables):
        hit = high == r
        for c, row in enumerate(rows):
            got = jnp.take_along_axis(
                jnp.broadcast_to(row, index.shape), low, axis=1, mode="promise_in_bounds"
            )
            found[c] = got if found[c] is None else jnp.where(hit, got, found[c])
    return found


def table_rows(refs, rows):
    return [[ref(r) for ref in refs] for r in range(rows)]


def scatter_tile(index, values, rows, pieces, live=None):
    high = index >> 7
    low = index & 127
    sublane = lax.broadcasted_iota(jnp.int32, (rows, L), 0)
    place = lax.broadcasted_iota(jnp.int32, (L, L), 0)
    left, right = [], []
    for s in range(live or index.shape[0]):
        mine = sublane == row_of(high, s, rows)
        stack = []
        for value in values:
            spread = jnp.where(mine, row_of(value, s, rows), 0.0)
            stack += split_pieces(spread, pieces)
        left.append(jnp.concatenate(stack, 0))
        right.append(jnp.where(place == row_of(low, s, L), 1.0, 0.0).astype(BF16))
    return lax.dot_general(
        jnp.concatenate(left, 1), jnp.concatenate(right, 1), NT, preferred_element_type=F32
    )


def unstack(total, count, rows, pieces):
    out = []
    for c in range(count):
        base = c * pieces * rows
        value = total[base : base + rows]
        for p in range(1, pieces):
            value = value + total[base + p * rows : base + (p + 1) * rows]
        out.append(value)
    return out


def advance(u, v, internal, received, shared, ext, mass, accel, rows, neighbours):
    added = unstack(scatter_tile(shared, received, rows, 3, neighbours), 3, rows, 3)
    assembled = [internal[c] + added[c] for c in range(3)]
    v = [v[c] + TIME_STEP * ((ext[c] - assembled[c]) / mass - accel[c]) for c in range(3)]
    u = [u[c] + TIME_STEP * v[c] for c in range(3)]
    return u, v, assembled


def elem_body(first, neighbours, *refs):
    if first:
        u_ref, v_ref, corner_ref, shared_ref, matrix_ref, out_ref, own_ref, field, total = refs
        u = [u_ref[c] for c in range(3)]
        v = [v_ref[c] for c in range(3)]
    else:
        (u_ref, v_ref, corner_ref, shared_ref, matrix_ref, int_ref, rec_ref, ext_ref, mass_ref,
         accel_ref, out_ref, own_ref, un_ref, vn_ref, field, total) = refs
        rows = u_ref.shape[1]
        u, v, _ = advance(
            [u_ref[c] for c in range(3)], [v_ref[c] for c in range(3)],
            [int_ref[c] for c in range(3)], [rec_ref[c] for c in range(3)], shared_ref[...],
            [ext_ref[c] for c in range(3)], mass_ref[...], [accel_ref[c] for c in range(3)],
            rows, neighbours)
        for c in range(3):
            un_ref[c] = u[c]
            vn_ref[c] = v[c]
    rows = u_ref.shape[1]
    for c in range(3):
        field[c] = u[c] + DAMP_RATIO * v[c]
    total[...] = jnp.zeros_like(total)
    blocks = corner_ref.shape[1] // L

    def step(b, carry):
        index = corner_ref[:, pl.ds(pl.multiple_of(b * L, L), L)]
        found = lookup(
            table_rows([lambda r, c=c: field[c, r : r + 1, :] for c in range(3)], rows), index)
        g = jnp.concatenate(found, 0)
        g_hi = g.astype(BF16).astype(F32)
        rhs = jnp.concatenate([g_hi, g - g_hi, g_hi, jnp.zeros((8, L), F32)], 0).astype(BF16)
        h = jnp.dot(matrix_ref[b], rhs, preferred_element_type=F32)
        total[...] += scatter_tile(index, [h[0:8], h[8:16], h[16:24]], rows, 2)
        return carry

    lax.fori_loop(0, blocks, step, 0, unroll=2)
    internal = unstack(total[...], 3, rows, 2)
    for c in range(3):
        out_ref[c] = internal[c]
        field[c] = internal[c]
    own = lookup(
        table_rows([lambda r, c=c: field[c, r : r + 1, :] for c in range(3)], rows),
        shared_ref[...])
    for c in range(3):
        own_ref[c] = own[c]


def slots_body(owner_ref, master_ref, normal_ref, slot_ref, pay_ref, *, domains, cap):
    tiles = owner_ref.shape[0]
    slot_rows = pay_ref.shape[1]
    domain = lax.broadcasted_iota(jnp.int32, (domains, L), 0)
    tri = (lax.broadcasted_iota(jnp.int32, (L, L), 0) <= lax.broadcasted_iota(
        jnp.int32, (L, L), 1)).astype(F32).astype(BF16)
    seen = jnp.zeros((domains, 1), F32)
    for t in range(tiles):
        owner = owner_ref[t : t + 1, :]
        hit = domain == jnp.broadcast_to(owner, (domains, L))
        hits = jnp.where(hit, 1.0, 0.0)
        upto = jnp.dot(hits.astype(BF16), tri, preferred_element_type=F32) + seen
        rank = jnp.sum(jnp.where(hit, upto, 0.0), axis=0, keepdims=True) - 1.0
        slot_ref[t : t + 1, :] = owner * cap + rank.astype(jnp.int32)
        seen = seen + jnp.sum(hits, axis=1, keepdims=True)
    acc = None
    for t in range(0, tiles, 8):
        sl = slice(t, t + 8)
        values = [normal_ref[c, sl, :] for c in range(3)] + [master_ref[sl, :].astype(F32) + 1.0]
        got = scatter_tile(slot_ref[sl, :], values, slot_rows, 3)
        acc = got if acc is None else acc + got
    for c, value in enumerate(unstack(acc, 4, slot_rows, 3)):
        pay_ref[c] = value


def project_body(neighbours, u_ref, v_ref, shared_ref, int_ref, rec_ref, ext_ref, mass_ref,
                 accel_ref, rest_ref, slave_ref, slot_ref, normal_ref, x_ref, vn_ref, as_ref,
                 pay_ref):
    rows = u_ref.shape[1]
    slot_rows = pay_ref.shape[1]
    u, v, assembled = advance(
        [u_ref[c] for c in range(3)], [v_ref[c] for c in range(3)],
        [int_ref[c] for c in range(3)], [rec_ref[c] for c in range(3)], shared_ref[...],
        [ext_ref[c] for c in range(3)], mass_ref[...], [accel_ref[c] for c in range(3)],
        rows, neighbours)
    for c in range(3):
        x_ref[c] = rest_ref[c] + u[c]
        vn_ref[c] = v[c]
        as_ref[c] = assembled[c]
    acc = None
    for t in range(0, slave_ref.shape[0], 8):
        sl = slice(t, t + 8)
        found = lookup(state_rows(x_ref, vn_ref, rows), slave_ref[sl, :])
        normal = [normal_ref[c, sl, :] for c in range(3)]
        along = sum(found[c] * normal[c] for c in range(3))
        speed = sum(found[3 + c] * normal[c] for c in range(3))
        got = scatter_tile(slot_ref[sl, :], [along, speed], slot_rows, 3)
        acc = got if acc is None else acc + got
    for c, value in enumerate(unstack(acc, 2, slot_rows, 3)):
        pay_ref[c] = value


def state_rows(x_ref, v_ref, rows):
    return table_rows(
        [lambda r, c=c: x_ref[c, r : r + 1, :] for c in range(3)]
        + [lambda r, c=c: v_ref[c, r : r + 1, :] for c in range(3)], rows)


def push_body(x_ref, v_ref, early_ref, late_ref, push_ref, force_ref, total):
    rows = x_ref.shape[1]
    total[...] = jnp.zeros_like(total)

    def step(i, carry):
        sl = pl.ds(pl.multiple_of(i * 8, 8), 8)
        coded = early_ref[3, sl, :]
        master = jnp.maximum(coded - 0.5, 0.0).astype(jnp.int32)
        normal = [early_ref[c, sl, :] for c in range(3)]
        found = lookup(state_rows(x_ref, v_ref, rows), master)
        gap = late_ref[0, sl, :] - sum(found[c] * normal[c] for c in range(3))
        closing = late_ref[1, sl, :] - sum(found[3 + c] * normal[c] for c in range(3))
        z = -gap / GAP_WIDTH
        soft = jnp.maximum(z, 0.0) + jnp.log1p(jnp.exp(-jnp.abs(z)))
        push = PENALTY * GAP_WIDTH * soft - CONTACT_DAMP * closing
        push = jnp.where(coded > 0.5, push, 0.0)
        push_ref[sl, :] = push
        total[...] += scatter_tile(master, [-push * normal[c] for c in range(3)], rows, 2)
        return carry

    lax.fori_loop(0, push_ref.shape[0] // 8, step, 0)
    for c, value in enumerate(unstack(total[...], 3, rows, 2)):
        force_ref[c] = value


def finish_body(x_ref, v_ref, as_ref, ext_ref, mass_ref, accel_ref, force_ref, push_ref, slot_ref,
                slave_ref, normal_ref, part_ref, nv_ref, sums_ref, vals, total):
    rows = x_ref.shape[1]
    push_rows = [[push_ref[r : r + 1, :]] for r in range(push_ref.shape[0])]
    acc = None
    for t in range(0, slave_ref.shape[0], 8):
        sl = slice(t, t + 8)
        push = lookup(push_rows, slot_ref[sl, :])[0]
        got = scatter_tile(slave_ref[sl, :], [push * normal_ref[c, sl, :] for c in range(3)],
                           rows, 2)
        acc = got if acc is None else acc + got
    slave_force = unstack(acc, 3, rows, 2)
    mass = mass_ref[...]
    x = [x_ref[c] for c in range(3)]
    net = []
    for c in range(3):
        force = force_ref[c] + slave_force[c]
        nv_ref[c] = v_ref[c] + TIME_STEP * force / mass
        net.append(ext_ref[c] - as_ref[c] + force - mass * accel_ref[c])
    turned = [x[1] * net[2] - x[2] * net[1], x[2] * net[0] - x[0] * net[2],
              x[0] * net[1] - x[1] * net[0]]
    for i, value in enumerate([mass] + [mass * x[c] for c in range(3)] + net + turned):
        vals[i] = value
    part_rows = sums_ref.shape[1]
    total[...] = jnp.zeros_like(total)

    def step(i, carry):
        sl = pl.ds(pl.multiple_of(i * 8, 8), 8)
        part = part_ref[sl, :]
        total[...] += scatter_tile(part, [vals[k, sl, :] for k in range(10)], part_rows, 3)
        return carry

    lax.fori_loop(0, rows // 8, step, 0)
    for k, value in enumerate(unstack(total[...], 10, part_rows, 3)):
        sums_ref[k] = value


VMEM = pl.BlockSpec(memory_space=pltpu.VMEM)
SMEM = pl.BlockSpec(memory_space=pltpu.SMEM)


def call(body, outs, scratch, specs, name):
    return pl.pallas_call(
        body,
        out_shape=outs,
        in_specs=specs,
        out_specs=[VMEM] * len(outs),
        scratch_shapes=scratch,
        name=name,
        compiler_params=pltpu.CompilerParams(vmem_limit_bytes=48 * 2**20),
    )


def cross_product(left, right):
    return jnp.stack([
        left[1] * right[2] - left[2] * right[1],
        left[2] * right[0] - left[0] * right[2],
        left[0] * right[1] - left[1] * right[0],
    ])


def partner(block, axis, apart):
    count = lax.axis_size(axis)
    route = []
    for low in range(count):
        high = low | 1 << apart
        if high != low and high < count:
            route += [(low, high), (high, low)]
    return lax.ppermute(block, axis, route)


def f32(*shape):
    return jax.ShapeDtypeStruct(shape, F32)


def swap(payload, domains, cap):
    count = payload.shape[0]
    return lax.all_to_all(
        payload.reshape(count, domains, cap), "dom", split_axis=1, concat_axis=1, tiled=True
    ).reshape(payload.shape)


def per_device(rest_pos, displacement, velocity, ext_force, node_mass, body_accel, connectivity,
               elem_material, stiffness, shared_nodes, contact_slave, contact_owner,
               contact_master, contact_normal, part_of_node, part_mass, part_center,
               part_inertia):
    domains = lax.axis_size("dom")
    neighbours, shared_count = shared_nodes.shape[1:]
    nodes = displacement.shape[1]
    rows = nodes // L
    elems = connectivity.shape[1]
    blocks = elems // L
    contacts = contact_slave.shape[0]
    tiles = contacts // L
    cap = -(-(4 * contacts // domains) // L) * L
    slot_rows = domains * cap // L
    part_rows = -(-PARTS_SIZE // L)

    corners = (connectivity + jnp.arange(elems, dtype=jnp.int32)[None, :]) % nodes
    u = displacement.reshape(3, rows, L)
    v = velocity.reshape(3, rows, L)
    ext = ext_force.reshape(3, rows, L)
    rest = rest_pos.reshape(3, rows, L)
    mass = node_mass.reshape(rows, L)
    shared = jnp.concatenate(
        [shared_nodes[0], jnp.zeros((8 - neighbours, shared_count), jnp.int32)], 0)
    k_hi = lax.reduce_precision(stiffness, 8, 7)
    k_lo = stiffness - k_hi
    matrix = jnp.concatenate(
        [k_hi, k_hi, k_lo, jnp.zeros(stiffness.shape[:2] + (8,), F32)], 2).astype(BF16)
    materials = stiffness.shape[0]
    pick = (elem_material[:, None] == jnp.arange(materials, dtype=jnp.int32)[None]).astype(BF16)
    matrix = jnp.dot(pick, matrix.reshape(materials, -1), preferred_element_type=F32)
    matrix = matrix.astype(BF16).reshape(blocks, 24, 80)

    owner = contact_owner.reshape(tiles, L)
    master = contact_master.reshape(tiles, L)
    slave = contact_slave.reshape(tiles, L)
    normal = contact_normal.reshape(3, tiles, L)
    slot, early = call(
        functools.partial(slots_body, domains=domains, cap=cap),
        [jax.ShapeDtypeStruct((tiles, L), jnp.int32), f32(4, slot_rows, L)], [],
        [VMEM] * 3, "slots")(owner, master, normal)
    early = swap(early, domains, cap)

    node_shape = f32(3, rows, L)
    own_shape = f32(3, 8, L)
    scratch = [pltpu.VMEM((3, rows, L), F32), pltpu.VMEM((6 * rows, L), F32)]
    received = internal = None
    for cycle in range(CYCLES):
        if cycle == 0:
            internal, own = call(
                functools.partial(elem_body, True, neighbours), [node_shape, own_shape], scratch,
                [VMEM] * 5, "elements")(u, v, corners, shared, matrix)
        else:
            internal, own, u, v = call(
                functools.partial(elem_body, False, neighbours),
                [node_shape, own_shape, node_shape, node_shape], scratch,
                [VMEM] * 9 + [SMEM], "elements")(
                    u, v, corners, shared, matrix, internal, received, ext, mass, body_accel)
        pieces = [partner(own[:, b], "dom", b) for b in range(neighbours)]
        received = jnp.stack(pieces + [jnp.zeros_like(pieces[0])] * (8 - neighbours), axis=1)

    x, v, assembled, late = call(
        functools.partial(project_body, neighbours),
        [node_shape, node_shape, node_shape, f32(2, slot_rows, L)], [],
        [VMEM] * 7 + [SMEM] + [VMEM] * 4, "project")(
            u, v, shared, internal, received, ext, mass, body_accel, rest, slave, slot, normal)
    late = swap(late, domains, cap)
    push, force = call(
        push_body, [f32(slot_rows, L), node_shape], [pltpu.VMEM((6 * rows, L), F32)],
        [VMEM] * 4, "push")(x, v, early, late)
    push = swap(push[None], domains, cap)[0]
    nodal_velocity, sums = call(
        finish_body, [node_shape, f32(10, part_rows, L)],
        [pltpu.VMEM((10, rows, L), F32), pltpu.VMEM((30 * part_rows, L), F32)],
        [VMEM] * 5 + [SMEM] + [VMEM] * 6, "finish")(
            x, v, assembled, ext, mass, body_accel, force, push, slot, slave, normal,
            part_of_node.reshape(rows, L))
    totals = lax.psum(sums, "dom").reshape(10, part_rows * L)[:, :PARTS_SIZE]
    mass_total = part_mass + totals[0]
    centre = (part_mass[None] * part_center + totals[1:4]) / mass_total[None]
    force_sum = totals[4:7]
    torque = totals[7:10] - cross_product(centre, force_sum)
    part_motion = jnp.concatenate([force_sum / mass_total[None], torque / part_inertia], 0)
    return nodal_velocity.reshape(3, nodes), part_motion


def solution(mesh):
    placed = (
        P(None, "dom"), P(None, "dom"), P(None, "dom"), P(None, "dom"), P("dom"), P(),
        P(None, "dom"), P("dom"), P(), P("dom", None, None), P("dom"), P("dom", None), P("dom"),
        P(None, "dom"), P("dom"), P(), P(), P(),
    )
    return jax.shard_map(
        per_device, mesh=mesh, in_specs=placed, out_specs=(P(None, "dom"), P()), check_vma=False
    )
```

time: 1270 us -> 160 us (0.13)
  other arithmetic: 656 us -> 1.73 us
  local copies, waits for them, and re-layouts: 507 us -> 7.6 us
  Pallas kernels: 0 us -> 57.3 us
    scatter-add x9 -> x0, other arithmetic: 638 us -> none  [the longest x3 524 us: element_forces(): return jnp.zeros_like(nodal_field).at[:, corners.reshape(-1)].add(forces....]
    gather x17 -> x0, local copies, waits for them, and re-layouts: 441 us -> none  [the longest x6 356 us: element_forces(): gathered = nodal_field[:, corners].reshape(24, blocks, 128)]
    pallas_call x0 -> x7, Pallas kernels: none -> 57.3 us  [the longest x2 32.2 us: per_device(): call(functools.partial(elem_body, False, neighbours), [node_shape, own_sh...]
    reshape x11 -> x8, local copies, waits for them, and re-layouts: 32.8 us -> 1.75 us  [the longest x4 1.48 us: swap(): payload.reshape(count, domains, cap)]
  transfers between devices with their start and end apart: 17 -> 17, of which waited for: 7 -> 5; matrix products, arithmetic and copies ran while one was open for 5% -> 1% of each run, Pallas kernels for 0% -> 1%
where the time goes in v1:
time: 160 us
  Pallas kernels  57.3 us (36%)
  blocking collectives  47.4 us (30%)
  starting transfers between devices  26 us (16%)
  waiting for transfers between devices  18.2 us (11%)
  local copies, waits for them, and re-layouts  7.6 us (5%)
  other arithmetic  1.73 us (1%)
    psum x1, blocking collectives, per_device(): totals = lax.psum(sums, 'dom').reshape(10, part_rows * L)[:, :PARTS_SIZE]  38.4 us
    pallas_call x2, Pallas kernels, per_device(): call(functools.partial(elem_body, False, neighbours), [node_shape, own_sh...  32.2 us
    ppermute x15, starting transfers between devices, partner(): return lax.ppermute(block, axis, route)  20.6 us
    pallas_call x1, Pallas kernels, per_device(): call(functools.partial(elem_body, True, neighbours), [node_shape, own_sha...  15.2 us
    all_to_all x2, waiting for transfers between devices, swap(): lax.all_to_all(payload.reshape(count, domains, cap), 'dom', split_axis=1,...  14.8 us
    all_to_all x1, blocking collectives, swap(): lax.all_to_all(payload.reshape(count, domains, cap), 'dom', split_axis=1,...  8.95 us
    unnamed x41, local copies, waits for them, and re-layouts  5.46 us
    all_to_all x2, starting transfers between devices, swap(): lax.all_to_all(payload.reshape(count, domains, cap), 'dom', split_axis=1,...  5.33 us
  transfers between devices with their start and end apart: 17, of which 5 were waited for; matrix products, arithmetic and copies ran while one was open for 1% of the time, Pallas kernels for 1%

profile of v1, /device:TPU:0, one launch (start us, length us, event | category | flops | bytes accessed | tf_op | source)
XLA Modules:
  0.0 159.5 jit_solution(4630335422514015841)
XLA Ops:
  0.6 0.9 reduce-precision_convert_fusion
  3.6 0.8 copy-done.7
  4.4 15.2 %elements.3 = (f32[3,32,128]{2,1,0:T(8,128)S(1)}, f32[3,8,128]{2,1,0:T(8,128)S(1)}) custom-call(f32[3,32,128]{2,1,0:T(8,128)S(1)} %get-tuple-element.65.refs_0_, f32[3,32,128]{2,1,0:T(8,128)S(1)} %get-tuple-element.64.refs_1_, s32[8,4096]{1,0:T(8,128)S(1)} %add_select_fusion.refs_2_, s32[8,128]{1,0:T(8,128)S(1)} %concatenate.10.refs_3_.shared_ref, ...), custom_call_target="tpu_custom_call" | custom-call | tf_op jit(solution)/shard_map/elements/pallas_call | solution.py:352
  20.3 2.6 %collective-permute-start.1 = (f32[3,128]{1,0:T(4,128)S(1)}, f32[3,128]{1,0:T(4,128)S(1)}, u32[]{:S(2)}, u32[]{:S(2)}) collective-permute-start(f32[3,128]{1,0:T(4,128)S(1)} %get-tuple-element.62), channel_id=1, source_target_pairs={{0,2},{2,0},{1,3},{3,1},{4,6},{6,4},{5,7},{7,5},{8,10},{10,8},{9,1... | collective-permute-start | bytes 4616 | tf_op jit(solution)/shard_map/ppermute | solution.py:289
  22.8 1.5 collective-permute-start.2
  24.4 1.6 collective-permute-start.3
  25.9 2.6 %collective-permute-start.4 = (f32[3,128]{1,0:T(4,128)S(1)}, f32[3,128]{1,0:T(4,128)S(1)}, u32[]{:S(2)}, u32[]{:S(2)}) collective-permute-start(f32[3,128]{1,0:T(4,128)S(1)} %get-tuple-element.59), channel_id=1, source_target_pairs={{0,16},{16,0},{1,17},{17,1},{2,18},{18,2},{3,19},{19,3},{4,20},{20... | collective-permute-start | bytes 4616 | tf_op jit(solution)/shard_map/ppermute | solution.py:289
  28.6 1.8 %collective-permute-done.4 = f32[3,128]{1,0:T(4,128)S(1)} collective-permute-done((f32[3,128]{1,0:T(4,128)S(1)}, f32[3,128]{1,0:T(4,128)S(1)}, u32[]{:S(2)}, u32[]{:S(2)}) %collective-permute-start.4) | collective-permute-done | bytes 1568 | tf_op jit(solution)/shard_map/ppermute | solution.py:289
  30.5 0.7 copy-done
  31.1 16.1 %elements.4 = (f32[3,32,128]{2,1,0:T(8,128)S(1)}, f32[3,8,128]{2,1,0:T(8,128)S(1)}, f32[3,32,128]{2,1,0:T(8,128)S(1)}, f32[3,32,128]{2,1,0:T(8,128)S(1)}) custom-call(f32[3,32,128]{2,1,0:T(8,128)S(1)} %get-tuple-element.65.refs_0_, f32[3,32,128]{2,1,0:T(8,128)S(1)} %get-tuple-element.64.refs_1_, s32[8,4096]{1,0:T(8,128)S(1)} %add_select_fusion.refs_2_, ...), custom_call_target="tpu_custom_call" | custom-call | tf_op jit(solution)/shard_map/elements/pallas_call | solution.py:356
  48.6 2.9 %collective-permute-start.9 = (f32[3,128]{1,0:T(4,128)S(1)}, f32[3,128]{1,0:T(4,128)S(1)}, u32[]{:S(2)}, u32[]{:S(2)}) collective-permute-start(f32[3,128]{1,0:T(4,128)S(1)} %get-tuple-element.54), channel_id=1, source_target_pairs={{0,16},{16,0},{1,17},{17,1},{2,18},{18,2},{3,19},{19,3},{4,20},{20... | collective-permute-start | bytes 4616 | tf_op jit(solution)/shard_map/ppermute | solution.py:289
  52.0 1.0 collective-permute-done.9
  53.1 16.1 %elements.5 = (f32[3,32,128]{2,1,0:T(8,128)S(1)}, f32[3,8,128]{2,1,0:T(8,128)S(1)}, f32[3,32,128]{2,1,0:T(8,128)S(1)}, f32[3,32,128]{2,1,0:T(8,128)S(1)}) custom-call(f32[3,32,128]{2,1,0:T(8,128)S(1)} %get-tuple-element.24.refs_0_, f32[3,32,128]{2,1,0:T(8,128)S(1)} %get-tuple-element.25.refs_1_, s32[8,4096]{1,0:T(8,128)S(1)} %add_select_fusion.refs_2_, ...), custom_call_target="tpu_custom_call" | custom-call | tf_op jit(solution)/shard_map/elements/pallas_call | solution.py:356
  69.3 1.9 %collective-permute-start.11 = (f32[3,128]{1,0:T(4,128)S(1)}, f32[3,128]{1,0:T(4,128)S(1)}, u32[]{:S(2)}, u32[]{:S(2)}) collective-permute-start(f32[3,128]{1,0:T(4,128)S(1)} %get-tuple-element.52), channel_id=1, source_target_pairs={{0,2},{2,0},{1,3},{3,1},{4,6},{6,4},{5,7},{7,5},{8,10},{10,8},{9,1... | collective-permute-start | bytes 4616 | tf_op jit(solution)/shard_map/ppermute | solution.py:289
  71.2 1.5 collective-permute-start.12
  72.7 1.6 collective-permute-start.13
  74.3 2.6 %collective-permute-start.14 = (f32[3,128]{1,0:T(4,128)S(1)}, f32[3,128]{1,0:T(4,128)S(1)}, u32[]{:S(2)}, u32[]{:S(2)}) collective-permute-start(f32[3,128]{1,0:T(4,128)S(1)} %get-tuple-element.49), channel_id=1, source_target_pairs={{0,16},{16,0},{1,17},{17,1},{2,18},{18,2},{3,19},{19,3},{4,20},{20... | collective-permute-start | bytes 4616 | tf_op jit(solution)/shard_map/ppermute | solution.py:289
  76.9 0.7 copy-done.4
  77.6 1.2 slots.1
  79.0 0.7 copy-done.1
  79.7 1.9 %project.1 = (f32[3,32,128]{2,1,0:T(8,128)S(1)}, f32[3,32,128]{2,1,0:T(8,128)S(1)}, f32[3,32,128]{2,1,0:T(8,128)S(1)}, f32[2,64,128]{2,1,0:T(8,128)S(1)}) custom-call(f32[3,32,128]{2,1,0:T(8,128)S(1)} %get-tuple-element.28.u_ref, f32[3,32,128]{2,1,0:T(8,128)S(1)} %get-tuple-element.29.v_ref, s32[8,128]{1,0:T(8,128)S(1)} %concatenate.10.refs_3_.shared_ref, ...), custom_call_target="tpu_custom_call" | custom-call | tf_op jit(solution)/shard_map/project/pallas_call | solution.py:364
  81.6 0.7 copy.52
  82.3 2.8 %all-to-all-start.1 = ((f32[2,32,256]{2,0,1:T(2,128)}), f32[2,32,256]{2,0,1:T(2,128)S(1)}, u32[]{:S(2)}, u32[]{:S(2)}) async-start(f32[2,32,256]{2,0,1:T(2,128)} %copy.52), calls=%async_computation.1 | async-start | bytes 131072 | tf_op jit(solution)/shard_map/all_to_all | solution.py:298
  85.1 0.7 copy.50
  85.8 6.6 %all-to-all-done.1 = f32[2,32,256]{2,0,1:T(2,128)S(1)} async-done(((f32[2,32,256]{2,0,1:T(2,128)}), f32[2,32,256]{2,0,1:T(2,128)S(1)}, u32[]{:S(2)}, u32[]{:S(2)}) %all-to-all-start.1) | async-done | bytes 65568 | tf_op jit(solution)/shard_map/all_to_all | solution.py:298
  92.4 2.6 %all-to-all-start = ((f32[4,32,256]{2,0,1:T(4,128)}), f32[4,32,256]{2,0,1:T(4,128)S(1)}, u32[]{:S(2)}, u32[]{:S(2)}) async-start(f32[4,32,256]{2,0,1:T(4,128)} %copy.50), calls=%async_computation | async-start | bytes 262144 | tf_op jit(solution)/shard_map/all_to_all | solution.py:298
  95.0 8.2 %all-to-all-done = f32[4,32,256]{2,0,1:T(4,128)S(1)} async-done(((f32[4,32,256]{2,0,1:T(4,128)}), f32[4,32,256]{2,0,1:T(4,128)S(1)}, u32[]{:S(2)}, u32[]{:S(2)}) %all-to-all-start) | async-done | bytes 131104 | tf_op jit(solution)/shard_map/all_to_all | solution.py:298
  103.3 4.4 %push.1 = (f32[64,128]{1,0:T(8,128)S(1)}, f32[3,32,128]{2,1,0:T(8,128)S(1)}) custom-call(f32[3,32,128]{2,1,0:T(8,128)S(1)} %get-tuple-element.33.x_ref, f32[3,32,128]{2,1,0:T(8,128)S(1)} %get-tuple-element.34.v_ref, f32[4,64,128]{2,1,0:T(8,128)S(1)} %reshape.72.early_ref, f32[2,64,128]{2,1,0:T(8,128)S(1)} %reshape.74.late_ref), custom_call_target="tpu_custom_call" | custom-call | tf_op jit(solution)/shard_map/push/pallas_call | solution.py:370
  107.7 9.0 %all_to_all.15 = f32[1,32,256]{2,0,1:T(1,128)S(1)} all-to-all(f32[1,32,256]{2,0,1:T(1,128)S(1)} %bitcast.83), channel_id=1, replica_groups=mesh['dom'=32] {'dom'}, dimensions={1} | all-to-all | bytes 65536 | tf_op jit(solution)/shard_map/all_to_all | solution.py:298
  116.6 2.4 %finish.1 = (f32[3,32,128]{2,1,0:T(8,128)S(1)}, f32[10,4,128]{2,1,0:T(4,128)S(1)}) custom-call(f32[3,32,128]{2,1,0:T(8,128)S(1)} %get-tuple-element.33.x_ref, f32[3,32,128]{2,1,0:T(8,128)S(1)} %get-tuple-element.34.v_ref, f32[3,32,128]{2,1,0:T(8,128)S(1)} %get-tuple-element.35.as_ref, f32[3,32,128]{2,1,0:T(8,128)S(1)} %bitcast.70, f32[32,128]{1,0:T(8,128)S(1)} %bitcast.77, ...), custom_call_target="tpu_custom_call" | custom-call | tf_op jit(solution)/shard_map/finish/pallas_call | solution.py:374
  119.0 38.4 %psum.7 = f32[10,512]{1,0:T(8,128)S(1)} all-reduce(f32[10,512]{1,0:T(8,128)S(1)} %bitcast.88), channel_id=1, replica_groups=mesh['dom'=32] {'dom'}, use_global_device_ids=true, to_apply=%region_0.1 | all-reduce | flops 5120 | bytes 40960 | tf_op jit(solution)/shard_map/psum | solution.py:380
  158.2 0.7 copy.70
  (102 shorter events, 6.3 us)
Async XLA Ops:
  2.6 0.7 copy-start.15
  2.6 0.9 copy-start.6
  3.5 0.8 copy-start.7
  3.6 0.9 copy-start.8
  4.4 24.1 %copy-start.9 = (f32[3,4096]{1,0:T(4,128)S(1)}, f32[3,4096]{1,0:T(4,128)}, u32[]{:S(2)}) copy-start(f32[3,4096]{1,0:T(4,128)} %param.21) | copy-start | bytes 147460
  19.7 8.8 %collective-permute-start = (f32[3,128]{1,0:T(4,128)S(1)}, f32[3,128]{1,0:T(4,128)S(1)}, u32[]{:S(2)}, u32[]{:S(2)}) collective-permute-start(f32[3,128]{1,0:T(4,128)S(1)} %get-tuple-element.63), channel_id=1, source_target_pairs={{0,1},{1,0},{2,3},{3,2},{4,5},{5,4},{6,7},{7,6},{8,9},{9,8},{10,11... | collective-permute-start | bytes 4616 | tf_op jit(solution)/shard_map/ppermute | solution.py:289
  20.3 8.3 %collective-permute-start.1 = (f32[3,128]{1,0:T(4,128)S(1)}, f32[3,128]{1,0:T(4,128)S(1)}, u32[]{:S(2)}, u32[]{:S(2)}) collective-permute-start(f32[3,128]{1,0:T(4,128)S(1)} %get-tuple-element.62), channel_id=1, source_target_pairs={{0,2},{2,0},{1,3},{3,1},{4,6},{6,4},{5,7},{7,5},{8,10},{10,8},{9,1... | collective-permute-start | bytes 4616 | tf_op jit(solution)/shard_map/ppermute | solution.py:289
  22.8 5.7 %collective-permute-start.2 = (f32[3,128]{1,0:T(4,128)S(1)}, f32[3,128]{1,0:T(4,128)S(1)}, u32[]{:S(2)}, u32[]{:S(2)}) collective-permute-start(f32[3,128]{1,0:T(4,128)S(1)} %get-tuple-element.61), channel_id=1, source_target_pairs={{0,4},{4,0},{1,5},{5,1},{2,6},{6,2},{3,7},{7,3},{8,12},{12,8},{9,1... | collective-permute-start | bytes 4616 | tf_op jit(solution)/shard_map/ppermute | solution.py:289
  24.4 4.2 %collective-permute-start.3 = (f32[3,128]{1,0:T(4,128)S(1)}, f32[3,128]{1,0:T(4,128)S(1)}, u32[]{:S(2)}, u32[]{:S(2)}) collective-permute-start(f32[3,128]{1,0:T(4,128)S(1)} %get-tuple-element.60), channel_id=1, source_target_pairs={{0,8},{8,0},{1,9},{9,1},{2,10},{10,2},{3,11},{11,3},{4,12},{12,4},... | collective-permute-start | bytes 4616 | tf_op jit(solution)/shard_map/ppermute | solution.py:289
  25.9 4.5 %collective-permute-start.4 = (f32[3,128]{1,0:T(4,128)S(1)}, f32[3,128]{1,0:T(4,128)S(1)}, u32[]{:S(2)}, u32[]{:S(2)}) collective-permute-start(f32[3,128]{1,0:T(4,128)S(1)} %get-tuple-element.59), channel_id=1, source_target_pairs={{0,16},{16,0},{1,17},{17,1},{2,18},{18,2},{3,19},{19,3},{4,20},{20... | collective-permute-start | bytes 4616 | tf_op jit(solution)/shard_map/ppermute | solution.py:289
  30.4 0.7 copy-start
  47.2 4.2 %collective-permute-start.5 = (f32[3,128]{1,0:T(4,128)S(1)}, f32[3,128]{1,0:T(4,128)S(1)}, u32[]{:S(2)}, u32[]{:S(2)}) collective-permute-start(f32[3,128]{1,0:T(4,128)S(1)} %get-tuple-element.58), channel_id=1, source_target_pairs={{0,1},{1,0},{2,3},{3,2},{4,5},{5,4},{6,7},{7,6},{8,9},{9,8},{10,11... | collective-permute-start | bytes 4616 | tf_op jit(solution)/shard_map/ppermute | solution.py:289
  47.3 4.2 %collective-permute-start.6 = (f32[3,128]{1,0:T(4,128)S(1)}, f32[3,128]{1,0:T(4,128)S(1)}, u32[]{:S(2)}, u32[]{:S(2)}) collective-permute-start(f32[3,128]{1,0:T(4,128)S(1)} %get-tuple-element.57), channel_id=1, source_target_pairs={{0,2},{2,0},{1,3},{3,1},{4,6},{6,4},{5,7},{7,5},{8,10},{10,8},{9,1... | collective-permute-start | bytes 4616 | tf_op jit(solution)/shard_map/ppermute | solution.py:289
  47.9 3.6 %collective-permute-start.7 = (f32[3,128]{1,0:T(4,128)S(1)}, f32[3,128]{1,0:T(4,128)S(1)}, u32[]{:S(2)}, u32[]{:S(2)}) collective-permute-start(f32[3,128]{1,0:T(4,128)S(1)} %get-tuple-element.56), channel_id=1, source_target_pairs={{0,4},{4,0},{1,5},{5,1},{2,6},{6,2},{3,7},{7,3},{8,12},{12,8},{9,1... | collective-permute-start | bytes 4616 | tf_op jit(solution)/shard_map/ppermute | solution.py:289
  48.4 3.6 %collective-permute-start.8 = (f32[3,128]{1,0:T(4,128)S(1)}, f32[3,128]{1,0:T(4,128)S(1)}, u32[]{:S(2)}, u32[]{:S(2)}) collective-permute-start(f32[3,128]{1,0:T(4,128)S(1)} %get-tuple-element.55), channel_id=1, source_target_pairs={{0,8},{8,0},{1,9},{9,1},{2,10},{10,2},{3,11},{11,3},{4,12},{12,4},... | collective-permute-start | bytes 4616 | tf_op jit(solution)/shard_map/ppermute | solution.py:289
  48.6 4.5 %collective-permute-start.9 = (f32[3,128]{1,0:T(4,128)S(1)}, f32[3,128]{1,0:T(4,128)S(1)}, u32[]{:S(2)}, u32[]{:S(2)}) collective-permute-start(f32[3,128]{1,0:T(4,128)S(1)} %get-tuple-element.54), channel_id=1, source_target_pairs={{0,16},{16,0},{1,17},{17,1},{2,18},{18,2},{3,19},{19,3},{4,20},{20... | collective-permute-start | bytes 4616 | tf_op jit(solution)/shard_map/ppermute | solution.py:289
  53.1 23.8 %copy-start.11 = (f32[3,2048]{1,0:T(4,128)S(1)}, f32[3,2048]{1,0:T(4,128)}, u32[]{:S(2)}) copy-start(f32[3,2048]{1,0:T(4,128)} %param.31) | copy-start | bytes 73732
  69.2 7.7 %copy-start.10 = (f32[3,4096]{1,0:T(4,128)S(1)}, f32[3,4096]{1,0:T(4,128)}, u32[]{:S(2)}) copy-start(f32[3,4096]{1,0:T(4,128)} %param.18) | copy-start | bytes 147460
  69.2 9.6 %collective-permute-start.10 = (f32[3,128]{1,0:T(4,128)S(1)}, f32[3,128]{1,0:T(4,128)S(1)}, u32[]{:S(2)}, u32[]{:S(2)}) collective-permute-start(f32[3,128]{1,0:T(4,128)S(1)} %get-tuple-element.53), channel_id=1, source_target_pairs={{0,1},{1,0},{2,3},{3,2},{4,5},{5,4},{6,7},{7,6},{8,9},{9,8},{10,11... | collective-permute-start | bytes 4616 | tf_op jit(solution)/shard_map/ppermute | solution.py:289
  69.3 9.6 %collective-permute-start.11 = (f32[3,128]{1,0:T(4,128)S(1)}, f32[3,128]{1,0:T(4,128)S(1)}, u32[]{:S(2)}, u32[]{:S(2)}) collective-permute-start(f32[3,128]{1,0:T(4,128)S(1)} %get-tuple-element.52), channel_id=1, source_target_pairs={{0,2},{2,0},{1,3},{3,1},{4,6},{6,4},{5,7},{7,5},{8,10},{10,8},{9,1... | collective-permute-start | bytes 4616 | tf_op jit(solution)/shard_map/ppermute | solution.py:289
  71.2 7.7 %collective-permute-start.12 = (f32[3,128]{1,0:T(4,128)S(1)}, f32[3,128]{1,0:T(4,128)S(1)}, u32[]{:S(2)}, u32[]{:S(2)}) collective-permute-start(f32[3,128]{1,0:T(4,128)S(1)} %get-tuple-element.51), channel_id=1, source_target_pairs={{0,4},{4,0},{1,5},{5,1},{2,6},{6,2},{3,7},{7,3},{8,12},{12,8},{9,1... | collective-permute-start | bytes 4616 | tf_op jit(solution)/shard_map/ppermute | solution.py:289
  72.7 6.2 %collective-permute-start.13 = (f32[3,128]{1,0:T(4,128)S(1)}, f32[3,128]{1,0:T(4,128)S(1)}, u32[]{:S(2)}, u32[]{:S(2)}) collective-permute-start(f32[3,128]{1,0:T(4,128)S(1)} %get-tuple-element.50), channel_id=1, source_target_pairs={{0,8},{8,0},{1,9},{9,1},{2,10},{10,2},{3,11},{11,3},{4,12},{12,4},... | collective-permute-start | bytes 4616 | tf_op jit(solution)/shard_map/ppermute | solution.py:289
  74.3 4.7 %collective-permute-start.14 = (f32[3,128]{1,0:T(4,128)S(1)}, f32[3,128]{1,0:T(4,128)S(1)}, u32[]{:S(2)}, u32[]{:S(2)}) collective-permute-start(f32[3,128]{1,0:T(4,128)S(1)} %get-tuple-element.49), channel_id=1, source_target_pairs={{0,16},{16,0},{1,17},{17,1},{2,18},{18,2},{3,19},{19,3},{4,20},{20... | collective-permute-start | bytes 4616 | tf_op jit(solution)/shard_map/ppermute | solution.py:289
  76.9 0.7 copy-start.4
  76.9 0.7 copy-start.5
  79.0 0.7 copy-start.1
  82.3 10.2 %all-to-all-start.1 = ((f32[2,32,256]{2,0,1:T(2,128)}), f32[2,32,256]{2,0,1:T(2,128)S(1)}, u32[]{:S(2)}, u32[]{:S(2)}) async-start(f32[2,32,256]{2,0,1:T(2,128)} %copy.52), calls=%async_computation.1 | async-start | bytes 131072 | tf_op jit(solution)/shard_map/all_to_all | solution.py:298
  92.4 10.8 %all-to-all-start = ((f32[4,32,256]{2,0,1:T(4,128)}), f32[4,32,256]{2,0,1:T(4,128)S(1)}, u32[]{:S(2)}, u32[]{:S(2)}) async-start(f32[4,32,256]{2,0,1:T(4,128)} %copy.50), calls=%async_computation | async-start | bytes 262144 | tf_op jit(solution)/shard_map/all_to_all | solution.py:298
  107.7 9.0 %copy-start.2 = (s32[4096]{0:T(1024)S(1)}, s32[4096]{0:T(1024)}, u32[]{:S(2)}) copy-start(s32[4096]{0:T(1024)} %param.32) | copy-start | bytes 49156
  157.4 0.7 copy-start.12
  157.4 0.7 copy-start.13
  158.2 0.7 copy-start.14
  (2 other events, 1.3 us)

commit v2 on v1

--- a/solution.py
+++ b/solution.py
@@ -61,7 +61,8 @@
         mine = sublane == row_of(high, s, rows)
         stack = []
         for value in values:
-            spread = jnp.where(mine, row_of(value, s, rows), 0.0)
+            row = value[s] if isinstance(value, list) else value[s : s + 1, :]
+            spread = jnp.where(mine, jnp.broadcast_to(row, (rows, L)), 0.0)
             stack += split_pieces(spread, pieces)
         left.append(jnp.concatenate(stack, 0))
         right.append(jnp.where(place == row_of(low, s, L), 1.0, 0.0).astype(BF16))
@@ -87,6 +88,10 @@
     v = [v[c] + TIME_STEP * ((ext[c] - assembled[c]) / mass - accel[c]) for c in range(3)]
     u = [u[c] + TIME_STEP * v[c] for c in range(3)]
     return u, v, assembled
+
+
+def by_part(rec_ref):
+    return [[rec_ref[b, c : c + 1, :] for b in range(rec_ref.shape[0])] for c in range(3)]
 
 
 def elem_body(first, neighbours, *refs):
@@ -100,7 +105,7 @@
         rows = u_ref.shape[1]
         u, v, _ = advance(
             [u_ref[c] for c in range(3)], [v_ref[c] for c in range(3)],
-            [int_ref[c] for c in range(3)], [rec_ref[c] for c in range(3)], shared_ref[...],
+            [int_ref[c] for c in range(3)], by_part(rec_ref), shared_ref[...],
             [ext_ref[c] for c in range(3)], mass_ref[...], [accel_ref[c] for c in range(3)],
             rows, neighbours)
         for c in range(3):
@@ -131,8 +136,9 @@
     own = lookup(
         table_rows([lambda r, c=c: field[c, r : r + 1, :] for c in range(3)], rows),
         shared_ref[...])
-    for c in range(3):
-        own_ref[c] = own[c]
+    for b in range(neighbours):
+        for c in range(3):
+            own_ref[b, c : c + 1, :] = own[c][b : b + 1, :]
 
 
 def slots_body(owner_ref, master_ref, normal_ref, slot_ref, pay_ref, *, domains, cap):
@@ -167,7 +173,7 @@
     slot_rows = pay_ref.shape[1]
     u, v, assembled = advance(
         [u_ref[c] for c in range(3)], [v_ref[c] for c in range(3)],
-        [int_ref[c] for c in range(3)], [rec_ref[c] for c in range(3)], shared_ref[...],
+        [int_ref[c] for c in range(3)], by_part(rec_ref), shared_ref[...],
         [ext_ref[c] for c in range(3)], mass_ref[...], [accel_ref[c] for c in range(3)],
         rows, neighbours)
     for c in range(3):
@@ -255,11 +261,122 @@
         sums_ref[k] = value
 
 
+def coords(index):
+    return {"dom": index}
+
+
+def greet(peers):
+    barrier = pltpu.get_barrier_semaphore()
+    for peer in peers:
+        pl.semaphore_signal(barrier, inc=1, device_id=coords(peer),
+                            device_id_type=pl.DeviceIdType.MESH)
+    pl.semaphore_wait(barrier, len(peers))
+
+
+def send(source, target, send_sem, recv_sem, peer):
+    return pltpu.make_async_remote_copy(
+        src_ref=source, dst_ref=target, send_sem=send_sem, recv_sem=recv_sem,
+        device_id=coords(peer), device_id_type=pl.DeviceIdType.MESH)
+
+
+def exchange_body(neighbours, own_ref, got_ref, send_sem, recv_sem):
+    me = lax.axis_index("dom")
+    peers = [me + (1 - 2 * ((me // 2**b) % 2)) * 2**b for b in range(neighbours)]
+    greet(peers)
+    copies = [send(own_ref.at[b], got_ref.at[b], send_sem.at[b], recv_sem.at[b], peers[b])
+              for b in range(neighbours)]
+    for copy in copies:
+        copy.start()
+    for copy in copies:
+        copy.wait()
+
+
+def swap_body(domains, in_ref, out_ref, send_sem, recv_sem, own_sem):
+    me = lax.axis_index("dom")
+    own = pltpu.make_async_copy(in_ref.at[me], out_ref.at[me], own_sem)
+    own.start()
+    barrier = pltpu.get_barrier_semaphore()
+
+    def peer_at(apart):
+        return (me + apart) % domains
+
+    def hello(apart, carry):
+        pl.semaphore_signal(barrier, inc=1, device_id=coords(peer_at(apart)),
+                            device_id_type=pl.DeviceIdType.MESH)
+        return carry
+
+    lax.fori_loop(1, domains, hello, 0)
+    pl.semaphore_wait(barrier, domains - 1)
+
+    def copy(apart):
+        peer = peer_at(apart)
+        return send(in_ref.at[peer], out_ref.at[me], send_sem.at[apart], recv_sem.at[apart], peer)
+
+    def begin(apart, carry):
+        copy(apart).start()
+        return carry
+
+    def end(apart, carry):
+        copy(apart).wait()
+        return carry
+
+    lax.fori_loop(1, domains, begin, 0)
+    lax.fori_loop(1, domains, end, 0)
+    own.wait()
+
+
+def bit_groups(domains):
+    bits = domains.bit_length() - 1
+    groups, low = [], 0
+    while low < bits:
+        width = min(3, bits - low)
+        if bits - low == 4:
+            width = 2
+        groups.append((low, width))
+        low += width
+    return groups
+
+
+def total_body(domains, in_ref, out_ref, *scratch):
+    groups = bit_groups(domains)
+    held, partial, (send_sem, recv_sem, own_sem) = (
+        scratch[:len(groups)], scratch[len(groups):2 * len(groups) - 1], scratch[-3:])
+    me = lax.axis_index("dom")
+    plans = []
+    for low, width in groups:
+        size = 2**width
+        digit = (me // 2**low) % size
+        base = me - digit * 2**low
+        plans.append((digit, [base + ((digit + o) % size) * 2**low for o in range(1, size)]))
+    greet([peer for _, peers in plans for peer in peers])
+    source = in_ref
+    place = 0
+    for g, (digit, peers) in enumerate(plans):
+        own = pltpu.make_async_copy(source, held[g].at[digit], own_sem.at[g])
+        copies = [own]
+        for i, peer in enumerate(peers):
+            copies.append(send(source, held[g].at[digit], send_sem.at[place + i],
+                               recv_sem.at[place + i], peer))
+        place += len(peers)
+        for copy in copies:
+            copy.start()
+        for copy in copies:
+            copy.wait()
+        value = held[g][0]
+        for k in range(1, len(peers) + 1):
+            value = value + held[g][k]
+        if g + 1 < len(plans):
+            partial[g][...] = value
+            source = partial[g]
+        else:
+            out_ref[...] = value
+
+
 VMEM = pl.BlockSpec(memory_space=pltpu.VMEM)
 SMEM = pl.BlockSpec(memory_space=pltpu.SMEM)
 
 
-def call(body, outs, scratch, specs, name):
+def call(body, outs, scratch, specs, name, collective=None):
     return pl.pallas_call(
         body,
         out_shape=outs,
@@ -267,7 +384,9 @@
         out_specs=[VMEM] * len(outs),
         scratch_shapes=scratch,
         name=name,
-        compiler_params=pltpu.CompilerParams(vmem_limit_bytes=48 * 2**20),
+        compiler_params=pltpu.CompilerParams(
+            vmem_limit_bytes=48 * 2**20, collective_id=collective,
+            has_side_effects=collective is not None),
     )
 
 
@@ -279,25 +398,47 @@
     ])
 
 
-def partner(block, axis, apart):
-    count = lax.axis_size(axis)
-    route = []
-    for low in range(count):
-        high = low | 1 << apart
-        if high != low and high < count:
-            route += [(low, high), (high, low)]
-    return lax.ppermute(block, axis, route)
-
-
 def f32(*shape):
     return jax.ShapeDtypeStruct(shape, F32)
 
 
-def swap(payload, domains, cap):
-    count = payload.shape[0]
-    return lax.all_to_all(
-        payload.reshape(count, domains, cap), "dom", split_axis=1, concat_axis=1, tiled=True
-    ).reshape(payload.shape)
+def by_owner(payload, domains):
+    count, slot_rows, _ = payload.shape
+    each = slot_rows // domains
+    return payload.reshape(count, domains, each, L).transpose(1, 0, 2, 3).reshape(
+        domains, count * each, L)
+
+
+def to_slots(payload, count):
+    domains, each, _ = payload.shape
+    each = each // count
+    return payload.reshape(domains, count, each, L).transpose(1, 0, 2, 3).reshape(
+        count, domains * each, L)
+
+
+def swap(payload, domains, collective):
+    return call(
+        functools.partial(swap_body, domains), [f32(*payload.shape)],
+        [pltpu.SemaphoreType.DMA((domains,))] * 2 + [pltpu.SemaphoreType.DMA], [VMEM], "swap",
+        collective)(payload)[0]
+
+
+def exchange(own):
+    neighbours = own.shape[0]
+    return call(
+        functools.partial(exchange_body, neighbours), [f32(*own.shape)],
+        [pltpu.SemaphoreType.DMA((neighbours,))] * 2, [VMEM], "exchange", 0)(own)[0]
+
+
+def total_over(sums, domains):
+    groups = bit_groups(domains)
+    count = sum(2**width - 1 for _, width in groups)
+    return call(
+        functools.partial(total_body, domains), [f32(*sums.shape)],
+        [pltpu.VMEM((2**width,) + sums.shape, F32) for _, width in groups]
+        + [pltpu.VMEM(sums.shape, F32)] * (len(groups) - 1)
+        + [pltpu.SemaphoreType.DMA((count,))] * 2 + [pltpu.SemaphoreType.DMA((len(groups),))],
+        [VMEM], "total", 1)(sums)[0]
 
 
 def per_device(rest_pos, displacement, velocity, ext_force, node_mass, body_accel, connectivity,
@@ -341,10 +482,10 @@
         functools.partial(slots_body, domains=domains, cap=cap),
         [jax.ShapeDtypeStruct((tiles, L), jnp.int32), f32(4, slot_rows, L)], [],
         [VMEM] * 3, "slots")(owner, master, normal)
-    early = swap(early, domains, cap)
+    early = to_slots(swap(by_owner(early, domains), domains, 2), 4)
 
     node_shape = f32(3, rows, L)
-    own_shape = f32(3, 8, L)
+    own_shape = f32(neighbours, 8, L)
     scratch = [pltpu.VMEM((3, rows, L), F32), pltpu.VMEM((6 * rows, L), F32)]
     received = internal = None
     for cycle in range(CYCLES):
@@ -358,26 +499,25 @@
                 [node_shape, own_shape, node_shape, node_shape], scratch,
                 [VMEM] * 9 + [SMEM], "elements")(
                     u, v, corners, shared, matrix, internal, received, ext, mass, body_accel)
-        pieces = [partner(own[:, b], "dom", b) for b in range(neighbours)]
-        received = jnp.stack(pieces + [jnp.zeros_like(pieces[0])] * (8 - neighbours), axis=1)
+        received = exchange(own)
 
     x, v, assembled, late = call(
         functools.partial(project_body, neighbours),
         [node_shape, node_shape, node_shape, f32(2, slot_rows, L)], [],
         [VMEM] * 7 + [SMEM] + [VMEM] * 4, "project")(
             u, v, shared, internal, received, ext, mass, body_accel, rest, slave, slot, normal)
-    late = swap(late, domains, cap)
+    late = to_slots(swap(by_owner(late, domains), domains, 3), 2)
     push, force = call(
         push_body, [f32(slot_rows, L), node_shape], [pltpu.VMEM((6 * rows, L), F32)],
         [VMEM] * 4, "push")(x, v, early, late)
-    push = swap(push[None], domains, cap)[0]
+    push = to_slots(swap(by_owner(push[None], domains), domains, 4), 1)[0]
     nodal_velocity, sums = call(
         finish_body, [node_shape, f32(10, part_rows, L)],
         [pltpu.VMEM((10, rows, L), F32), pltpu.VMEM((30 * part_rows, L), F32)],
         [VMEM] * 5 + [SMEM] + [VMEM] * 6, "finish")(
             x, v, assembled, ext, mass, body_accel, force, push, slot, slave, normal,
             part_of_node.reshape(rows, L))
-    totals = lax.psum(sums, "dom").reshape(10, part_rows * L)[:, :PARTS_SIZE]
+    totals = total_over(sums, domains).reshape(10, part_rows * L)[:, :PARTS_SIZE]
     mass_total = part_mass + totals[0]
     centre = (part_mass[None] * part_center + totals[1:4]) / mass_total[None]
     force_sum = totals[4:7]

time: 160 us -> 119 us (0.74)
  Pallas kernels: 57.3 us -> 110 us
  blocking collectives: 47.4 us -> 0 us
  starting transfers between devices: 26 us -> 0 us
  waiting for transfers between devices: 18.2 us -> 0 us
    pallas_call x0 -> x7, Pallas kernels: none -> 52.4 us  [the longest x3 25.2 us: swap(): call(functools.partial(swap_body, domains), [f32(*payload.shape)], [pltpu...]
    psum x1 -> x0, blocking collectives: 38.4 us -> none  [per_device(): totals = lax.psum(sums, 'dom').reshape(10, part_rows * L)[:, :PARTS_SIZE]]
    ppermute x15 -> x0, starting transfers between devices: 20.6 us -> none  [partner(): return lax.ppermute(block, axis, route)]
    all_to_all x2 -> x0, waiting for transfers between devices: 14.8 us -> none  [swap(): lax.all_to_all(payload.reshape(count, domains, cap), 'dom', split_axis=1,...]
    all_to_all x1 -> x0, blocking collectives: 8.95 us -> none  [swap(): lax.all_to_all(payload.reshape(count, domains, cap), 'dom', split_axis=1,...]
    all_to_all x2 -> x0, starting transfers between devices: 5.33 us -> none  [swap(): lax.all_to_all(payload.reshape(count, domains, cap), 'dom', split_axis=1,...]
    ppermute x15 -> x0, waiting for transfers between devices: 3.39 us -> none  [partner(): return lax.ppermute(block, axis, route)]
    unnamed x41 -> x39, local copies, waits for them, and re-layouts: 5.46 us -> 5.43 us
  transfers between devices with their start and end apart: 17 -> 0, of which waited for: 5 -> 0; matrix products, arithmetic and copies ran while one was open for 1% -> 0% of each run, Pallas kernels for 1% -> 0%
where the time goes in v2:
time: 119 us
  Pallas kernels  110 us (92%)
  local copies, waits for them, and re-layouts  6.03 us (5%)
  other arithmetic  1.73 us (1%)
    pallas_call x2, Pallas kernels, per_device(): call(functools.partial(elem_body, False, neighbours), [node_shape, own_sh...  32.1 us
    pallas_call x3, Pallas kernels, swap(): call(functools.partial(swap_body, domains), [f32(*payload.shape)], [pltpu...  25.2 us
    pallas_call x3, Pallas kernels, exchange(): call(functools.partial(exchange_body, neighbours), [f32(*own.shape)], [pl...  16.9 us
    pallas_call x1, Pallas kernels, per_device(): call(functools.partial(elem_body, True, neighbours), [node_shape, own_sha...  15.3 us
    pallas_call x1, Pallas kernels, total_over(): call(functools.partial(total_body, domains), [f32(*sums.shape)], [pltpu.V...  10.3 us
    unnamed x39, local copies, waits for them, and re-layouts  5.43 us
    pallas_call x1, Pallas kernels, per_device(): call(push_body, [f32(slot_rows, L), node_shape], [pltpu.VMEM((6 * rows, L...  4.38 us

profile of v2, /device:TPU:0, one launch (start us, length us, event | category | flops | bytes accessed | tf_op | source)
XLA Modules:
  0.0 118.6 jit_solution(1906356688945009422)
XLA Ops:
  0.6 0.9 reduce-precision_convert_fusion
  1.6 0.1 pad.9.clone
  1.6 0.1 maximum_maximum_fusion
  1.7 0.1 convert_element_type.9
  1.9 0.5 copy-done.16
  2.4 0.2 convolution_convert_fusion
  2.7 0.2 reshape.75.refs_4_
  2.9 0.4 copy-done.15
  3.3 0.2 copy-done.6
  3.6 0.1 add_select_fusion.refs_2_
  3.6 0.8 copy-done.7
  4.4 0.0 copy-done.8
  4.4 15.3 %elements.3 = (f32[3,32,128]{2,1,0:T(8,128)S(1)}, f32[5,8,128]{2,1,0:T(8,128)S(1)}) custom-call(f32[3,32,128]{2,1,0:T(8,128)S(1)} %get-tuple-element.50.refs_0_, f32[3,32,128]{2,1,0:T(8,128)S(1)} %get-tuple-element.49.refs_1_, s32[8,4096]{1,0:T(8,128)S(1)} %add_select_fusion.refs_2_, s32[8,128]{1,0:T(8,128)S(1)} %concatenate.10.refs_3_.shared_ref, ...), custom_call_target="tpu_custom_call" | custom-call | tf_op jit(solution)/shard_map/elements/pallas_call | solution.py:493
  19.7 7.4 %exchange.3.refs_6_ = f32[5,8,128]{2,1,0:T(8,128)S(1)} custom-call(f32[5,8,128]{2,1,0:T(8,128)S(1)} %get-tuple-element.23.own_ref), custom_call_target="tpu_custom_call" | custom-call | tf_op jit(solution)/shard_map/exchange/pallas_call | solution.py:428
  27.2 0.7 copy-done
  27.9 16.1 %elements.4 = (f32[3,32,128]{2,1,0:T(8,128)S(1)}, f32[5,8,128]{2,1,0:T(8,128)S(1)}, f32[3,32,128]{2,1,0:T(8,128)S(1)}, f32[3,32,128]{2,1,0:T(8,128)S(1)}) custom-call(f32[3,32,128]{2,1,0:T(8,128)S(1)} %get-tuple-element.50.refs_0_, f32[3,32,128]{2,1,0:T(8,128)S(1)} %get-tuple-element.49.refs_1_, s32[8,4096]{1,0:T(8,128)S(1)} %add_select_fusion.refs_2_, ...), custom_call_target="tpu_custom_call" | custom-call | tf_op jit(solution)/shard_map/elements/pallas_call | solution.py:497
  43.9 4.7 %exchange.4.refs_6_ = f32[5,8,128]{2,1,0:T(8,128)S(1)} custom-call(f32[5,8,128]{2,1,0:T(8,128)S(1)} %get-tuple-element.27.own_ref), custom_call_target="tpu_custom_call" | custom-call | tf_op jit(solution)/shard_map/exchange/pallas_call | solution.py:428
  48.7 16.1 %elements.5 = (f32[3,32,128]{2,1,0:T(8,128)S(1)}, f32[5,8,128]{2,1,0:T(8,128)S(1)}, f32[3,32,128]{2,1,0:T(8,128)S(1)}, f32[3,32,128]{2,1,0:T(8,128)S(1)}) custom-call(f32[3,32,128]{2,1,0:T(8,128)S(1)} %get-tuple-element.24.refs_0_, f32[3,32,128]{2,1,0:T(8,128)S(1)} %get-tuple-element.25.refs_1_, s32[8,4096]{1,0:T(8,128)S(1)} %add_select_fusion.refs_2_, ...), custom_call_target="tpu_custom_call" | custom-call | tf_op jit(solution)/shard_map/elements/pallas_call | solution.py:497
  64.8 4.7 %exchange.5.rec_ref = f32[5,8,128]{2,1,0:T(8,128)S(1)} custom-call(f32[5,8,128]{2,1,0:T(8,128)S(1)} %get-tuple-element.31.own_ref), custom_call_target="tpu_custom_call" | custom-call | tf_op jit(solution)/shard_map/exchange/pallas_call | solution.py:428
  69.6 0.7 copy-done.4
  70.2 1.2 %slots.1 = (s32[16,128]{1,0:T(8,128)S(1)}, f32[4,64,128]{2,1,0:T(8,128)S(1)}) custom-call(s32[16,128]{1,0:T(8,128)S(1)} %bitcast.72, s32[16,128]{1,0:T(8,128)S(1)} %bitcast.73, f32[3,16,128]{2,1,0:T(8,128)S(1)} %bitcast.54), custom_call_target="tpu_custom_call" | custom-call | tf_op jit(solution)/shard_map/slots/pallas_call | solution.py:481
  71.5 1.9 %project.1 = (f32[3,32,128]{2,1,0:T(8,128)S(1)}, f32[3,32,128]{2,1,0:T(8,128)S(1)}, f32[3,32,128]{2,1,0:T(8,128)S(1)}, f32[2,64,128]{2,1,0:T(8,128)S(1)}) custom-call(f32[3,32,128]{2,1,0:T(8,128)S(1)} %get-tuple-element.28.u_ref, f32[3,32,128]{2,1,0:T(8,128)S(1)} %get-tuple-element.29.v_ref, s32[8,128]{1,0:T(8,128)S(1)} %concatenate.10.refs_3_.shared_ref, ...), custom_call_target="tpu_custom_call" | custom-call | tf_op jit(solution)/shard_map/project/pallas_call | solution.py:504
  73.4 8.3 %swap.4 = f32[32,4,128]{2,1,0:T(4,128)S(1)} custom-call(f32[32,4,128]{2,1,0:T(4,128)S(1)} %bitcast.61), custom_call_target="tpu_custom_call" | custom-call | tf_op jit(solution)/shard_map/swap/pallas_call | solution.py:420
  81.8 8.5 %swap.3 = f32[32,8,128]{2,1,0:T(8,128)S(1)} custom-call(f32[32,8,128]{2,1,0:T(8,128)S(1)} %bitcast.52), custom_call_target="tpu_custom_call" | custom-call | tf_op jit(solution)/shard_map/swap/pallas_call | solution.py:420
  90.4 4.4 %push.1 = (f32[64,128]{1,0:T(8,128)S(1)}, f32[3,32,128]{2,1,0:T(8,128)S(1)}) custom-call(f32[3,32,128]{2,1,0:T(8,128)S(1)} %get-tuple-element.33.x_ref, f32[3,32,128]{2,1,0:T(8,128)S(1)} %get-tuple-element.34.v_ref, f32[4,64,128]{2,1,0:T(8,128)S(1)} %bitcast.51, f32[2,64,128]{2,1,0:T(8,128)S(1)} %bitcast.63), custom_call_target="tpu_custom_call" | custom-call | tf_op jit(solution)/shard_map/push/pallas_call | solution.py:510
  94.8 8.3 %swap.5 = f32[32,2,128]{2,1,0:T(2,128)S(1)} custom-call(f32[32,2,128]{2,1,0:T(2,128)S(1)} %bitcast.70), custom_call_target="tpu_custom_call" | custom-call | tf_op jit(solution)/shard_map/swap/pallas_call | solution.py:420
  103.2 2.4 %finish.1 = (f32[3,32,128]{2,1,0:T(8,128)S(1)}, f32[10,4,128]{2,1,0:T(4,128)S(1)}) custom-call(f32[3,32,128]{2,1,0:T(8,128)S(1)} %get-tuple-element.33.x_ref, f32[3,32,128]{2,1,0:T(8,128)S(1)} %get-tuple-element.34.v_ref, f32[3,32,128]{2,1,0:T(8,128)S(1)} %get-tuple-element.35.as_ref, f32[3,32,128]{2,1,0:T(8,128)S(1)} %get-tuple-element.52.refs_7_.ext_ref, ...), custom_call_target="tpu_custom_call" | custom-call | tf_op jit(solution)/shard_map/finish/pallas_call | solution.py:514
  105.6 10.3 %total.1 = f32[10,4,128]{2,1,0:T(4,128)S(1)} custom-call(f32[10,4,128]{2,1,0:T(4,128)S(1)} %get-tuple-element.41.in_ref), custom_call_target="tpu_custom_call" | custom-call | tf_op jit(solution)/shard_map/total/pallas_call | solution.py:436
  116.0 0.6 copy-done.12
  116.7 0.7 copy-done.14
  117.4 0.6 pad_maximum_fusion
  118.0 0.7 copy.39
  (42 shorter events, 0.4 us)
Async XLA Ops:
  1.7 0.7 copy-start.16
  2.6 0.7 copy-start.15
  2.6 0.9 copy-start.6
  3.5 0.8 copy-start.7
  3.6 0.9 copy-start.8
  4.4 22.7 %copy-start.9 = (f32[3,4096]{1,0:T(4,128)S(1)}, f32[3,4096]{1,0:T(4,128)}, u32[]{:S(2)}) copy-start(f32[3,4096]{1,0:T(4,128)} %param.18) | copy-start | bytes 147460
  4.4 22.7 %copy-start.10 = (f32[3,4096]{1,0:T(4,128)S(1)}, f32[3,4096]{1,0:T(4,128)}, u32[]{:S(2)}) copy-start(f32[3,4096]{1,0:T(4,128)} %param.21) | copy-start | bytes 147460
  27.1 0.7 copy-start
  27.2 0.7 copy-start.3
  64.8 4.7 %copy-start.11 = (f32[3,2048]{1,0:T(4,128)S(1)}, f32[3,2048]{1,0:T(4,128)}, u32[]{:S(2)}) copy-start(f32[3,2048]{1,0:T(4,128)} %param.31) | copy-start | bytes 73732
  69.5 0.7 copy-start.4
  69.5 0.7 copy-start.5
  70.2 1.2 %copy-start.1 = (s32[2048]{0:T(1024)S(1)}, s32[2048]{0:T(1024)}, u32[]{:S(2)}) copy-start(s32[2048]{0:T(1024)} %param.28) | copy-start | bytes 24580
  94.8 8.4 %copy-start.2 = (s32[4096]{0:T(1024)S(1)}, s32[4096]{0:T(1024)}, u32[]{:S(2)}) copy-start(s32[4096]{0:T(1024)} %param.32) | copy-start | bytes 49156
  115.9 0.7 copy-start.12
  115.9 0.7 copy-start.13
  116.6 0.7 copy-start.14

commit v3 on v2

--- a/solution.py
+++ b/solution.py
@@ -15,22 +15,10 @@
 GAP_WIDTH = 0.5
 CONTACT_DAMP = 0.2
 L = 128
+GROUP = 4
 F32 = jnp.float32
 BF16 = jnp.bfloat16
 NT = (((1,), (1,)), ((), ()))
-
-
-def split_pieces(value, pieces):
-    out = []
-    for _ in range(pieces):
-        piece = value.astype(BF16)
-        out.append(piece)
-        value = value - piece.astype(F32)
-    return out
-
-
-def row_of(value, row, count):
-    return jnp.broadcast_to(value[row : row + 1, :], (count, L))
 
 
 def lookup(tables, index):
@@ -52,20 +40,29 @@
 
 
 def scatter_tile(index, values, rows, pieces, live=None):
-    high = index >> 7
-    low = index & 127
-    sublane = lax.broadcasted_iota(jnp.int32, (rows, L), 0)
-    place = lax.broadcasted_iota(jnp.int32, (L, L), 0)
+    high = (index >> 7).astype(F32)
+    low = (index & 127).astype(F32)
+    sublane = lax.broadcasted_iota(jnp.int32, (max(rows, 16), L), 0).astype(F32).astype(BF16)
+    place = lax.broadcasted_iota(jnp.int32, (L, L), 0).astype(F32).astype(BF16)
+    one, zero = jnp.ones((), BF16), jnp.zeros((), BF16)
+    parts = []
+    for value in values:
+        value = jnp.concatenate(value, 0) if isinstance(value, list) else value
+        for p in range(pieces):
+            piece = value.astype(BF16).astype(F32) if p + 1 < pieces else value
+            parts.append(piece)
+            value = value - piece
     left, right = [], []
+
+    def spread(value, s, count):
+        row = jnp.broadcast_to(value[s : s + 1, :], (16, L)).astype(BF16)
+        return jnp.concatenate([row] * (count // 16), 0) if count > 16 else row
+
     for s in range(live or index.shape[0]):
-        mine = sublane == row_of(high, s, rows)
-        stack = []
-        for value in values:
-            row = value[s] if isinstance(value, list) else value[s : s + 1, :]
-            spread = jnp.where(mine, jnp.broadcast_to(row, (rows, L)), 0.0)
-            stack += split_pieces(spread, pieces)
-        left.append(jnp.concatenate(stack, 0))
-        right.append(jnp.where(place == row_of(low, s, L), 1.0, 0.0).astype(BF16))
+        mine = sublane == spread(high, s, sublane.shape[0])
+        left.append(jnp.concatenate(
+            [jnp.where(mine, spread(part, s, sublane.shape[0]), zero) for part in parts], 0))
+        right.append(jnp.where(place == spread(low, s, L), one, zero))
     return lax.dot_general(
         jnp.concatenate(left, 1), jnp.concatenate(right, 1), NT, preferred_element_type=F32
     )
@@ -73,11 +70,12 @@
 
 def unstack(total, count, rows, pieces):
     out = []
+    step = max(rows, 16)
     for c in range(count):
-        base = c * pieces * rows
+        base = c * pieces * step
         value = total[base : base + rows]
         for p in range(1, pieces):
-            value = value + total[base + p * rows : base + (p + 1) * rows]
+            value = value + total[base + p * step : base + p * step + rows]
         out.append(value)
     return out
 
@@ -117,18 +115,34 @@
     total[...] = jnp.zeros_like(total)
     blocks = corner_ref.shape[1] // L
 
-    def step(b, carry):
-        index = corner_ref[:, pl.ds(pl.multiple_of(b * L, L), L)]
+    def corner_index(b):
+        return corner_ref[:, pl.ds(pl.multiple_of(b * L, L), L)]
+
+    def forces(b):
         found = lookup(
-            table_rows([lambda r, c=c: field[c, r : r + 1, :] for c in range(3)], rows), index)
+            table_rows([lambda r, c=c: field[c, r : r + 1, :] for c in range(3)], rows),
+            corner_index(b))
         g = jnp.concatenate(found, 0)
         g_hi = g.astype(BF16).astype(F32)
         rhs = jnp.concatenate([g_hi, g - g_hi, g_hi, jnp.zeros((8, L), F32)], 0).astype(BF16)
         h = jnp.dot(matrix_ref[b], rhs, preferred_element_type=F32)
-        total[...] += scatter_tile(index, [h[0:8], h[8:16], h[16:24]], rows, 2)
-        return carry
-
-    lax.fori_loop(0, blocks, step, 0, unroll=2)
+        return h[0:8], h[8:16], h[16:24]
+
+    def group(i):
+        each = [forces(i * GROUP + k) for k in range(GROUP)]
+        return tuple(jnp.concatenate([h[c] for h in each], 0) for c in range(3))
+
+    def add_group(i, held):
+        index = jnp.concatenate([corner_index(i * GROUP + k) for k in range(GROUP)], 0)
+        total[...] += scatter_tile(index, list(held), rows, 2)
+
+    def step(i, held):
+        coming = group(i)
+        add_group(i - 1, held)
+        return coming
+
+    groups = blocks // GROUP
+    add_group(groups - 1, lax.fori_loop(1, groups, step, group(0)))
     internal = unstack(total[...], 3, rows, 2)
     for c in range(3):
         out_ref[c] = internal[c]
@@ -199,18 +213,18 @@
         + [lambda r, c=c: v_ref[c, r : r + 1, :] for c in range(3)], rows)
 
 
-def push_body(x_ref, v_ref, early_ref, late_ref, push_ref, force_ref, total):
+def push_body(x_ref, v_ref, sent_ref, push_ref, force_ref, total):
     rows = x_ref.shape[1]
     total[...] = jnp.zeros_like(total)
 
     def step(i, carry):
         sl = pl.ds(pl.multiple_of(i * 8, 8), 8)
-        coded = early_ref[3, sl, :]
+        coded = sent_ref[3, sl, :]
         master = jnp.maximum(coded - 0.5, 0.0).astype(jnp.int32)
-        normal = [early_ref[c, sl, :] for c in range(3)]
+        normal = [sent_ref[c, sl, :] for c in range(3)]
         found = lookup(state_rows(x_ref, v_ref, rows), master)
-        gap = late_ref[0, sl, :] - sum(found[c] * normal[c] for c in range(3))
-        closing = late_ref[1, sl, :] - sum(found[3 + c] * normal[c] for c in range(3))
+        gap = sent_ref[4, sl, :] - sum(found[c] * normal[c] for c in range(3))
+        closing = sent_ref[5, sl, :] - sum(found[3 + c] * normal[c] for c in range(3))
         z = -gap / GAP_WIDTH
         soft = jnp.maximum(z, 0.0) + jnp.log1p(jnp.exp(-jnp.abs(z)))
         push = PENALTY * GAP_WIDTH * soft - CONTACT_DAMP * closing
@@ -295,33 +309,14 @@
     me = lax.axis_index("dom")
     own = pltpu.make_async_copy(in_ref.at[me], out_ref.at[me], own_sem)
     own.start()
-    barrier = pltpu.get_barrier_semaphore()
-
-    def peer_at(apart):
-        return (me + apart) % domains
-
-    def hello(apart, carry):
-        pl.semaphore_signal(barrier, inc=1, device_id=coords(peer_at(apart)),
-                            device_id_type=pl.DeviceIdType.MESH)
-        return carry
-
-    lax.fori_loop(1, domains, hello, 0)
-    pl.semaphore_wait(barrier, domains - 1)
-
-    def copy(apart):
-        peer = peer_at(apart)
-        return send(in_ref.at[peer], out_ref.at[me], send_sem.at[apart], recv_sem.at[apart], peer)
-
-    def begin(apart, carry):
-        copy(apart).start()
-        return carry
-
-    def end(apart, carry):
-        copy(apart).wait()
-        return carry
-
-    lax.fori_loop(1, domains, begin, 0)
-    lax.fori_loop(1, domains, end, 0)
+    peers = [(me + apart) % domains for apart in range(1, domains)]
+    greet(peers)
+    copies = [send(in_ref.at[peer], out_ref.at[me], send_sem.at[i], recv_sem.at[i], peer)
+              for i, peer in enumerate(peers)]
+    for copy in copies:
+        copy.start()
+    for copy in copies:
+        copy.wait()
     own.wait()
 
 
@@ -482,7 +477,6 @@
         functools.partial(slots_body, domains=domains, cap=cap),
         [jax.ShapeDtypeStruct((tiles, L), jnp.int32), f32(4, slot_rows, L)], [],
         [VMEM] * 3, "slots")(owner, master, normal)
-    early = to_slots(swap(by_owner(early, domains), domains, 2), 4)
 
     node_shape = f32(3, rows, L)
     own_shape = f32(neighbours, 8, L)
@@ -506,14 +500,15 @@
         [node_shape, node_shape, node_shape, f32(2, slot_rows, L)], [],
         [VMEM] * 7 + [SMEM] + [VMEM] * 4, "project")(
             u, v, shared, internal, received, ext, mass, body_accel, rest, slave, slot, normal)
-    late = to_slots(swap(by_owner(late, domains), domains, 3), 2)
+    sent = jnp.concatenate([early, late], 0)
+    sent = to_slots(swap(by_owner(sent, domains), domains, 3), 6)
     push, force = call(
         push_body, [f32(slot_rows, L), node_shape], [pltpu.VMEM((6 * rows, L), F32)],
-        [VMEM] * 4, "push")(x, v, early, late)
+        [VMEM] * 3, "push")(x, v, sent)
     push = to_slots(swap(by_owner(push[None], domains), domains, 4), 1)[0]
     nodal_velocity, sums = call(
         finish_body, [node_shape, f32(10, part_rows, L)],
-        [pltpu.VMEM((10, rows, L), F32), pltpu.VMEM((30 * part_rows, L), F32)],
+        [pltpu.VMEM((10, rows, L), F32), pltpu.VMEM((30 * max(part_rows, 16), L), F32)],
         [VMEM] * 5 + [SMEM] + [VMEM] * 6, "finish")(
             x, v, assembled, ext, mass, body_accel, force, push, slot, slave, normal,
             part_of_node.reshape(rows, L))

time: 119 us -> 98.9 us (0.83)
  Pallas kernels: 110 us -> 89.1 us
    pallas_call x2, Pallas kernels: 32.1 us -> 22.9 us  [per_device(): call(functools.partial(elem_body, False, neighbours), [node_shape, own_sh...]
    pallas_call x3 -> x2, Pallas kernels: 25.2 us -> 18.1 us  [swap(): call(functools.partial(swap_body, domains), [f32(*payload.shape)], [pltpu...]
    pallas_call x1, Pallas kernels: 15.3 us -> 10.6 us  [per_device(): call(functools.partial(elem_body, True, neighbours), [node_shape, own_sha...]
where the time goes in v3:
time: 98.9 us; the launch traced here: 98.3 us
  Pallas kernels  89.1 us (90%)
  local copies, waits for them, and re-layouts  6.25 us (6%)
  other arithmetic  1.75 us (2%)
  between operations  1.01 us (1%)
    pallas_call x2, Pallas kernels, per_device(): call(functools.partial(elem_body, False, neighbours), [node_shape, own_sh...  22.9 us
    pallas_call x2, Pallas kernels, swap(): call(functools.partial(swap_body, domains), [f32(*payload.shape)], [pltpu...  18.1 us
    pallas_call x3, Pallas kernels, exchange(): call(functools.partial(exchange_body, neighbours), [f32(*own.shape)], [pl...  16.9 us
    pallas_call x1, Pallas kernels, per_device(): call(functools.partial(elem_body, True, neighbours), [node_shape, own_sha...  10.6 us
    pallas_call x1, Pallas kernels, total_over(): call(functools.partial(total_body, domains), [f32(*sums.shape)], [pltpu.V...  10.5 us
    unnamed x39, local copies, waits for them, and re-layouts  5.43 us
    pallas_call x1, Pallas kernels, per_device(): call(push_body, [f32(slot_rows, L), node_shape], [pltpu.VMEM((6 * rows, L...  4.21 us
    pallas_call x1, Pallas kernels, per_device(): call(finish_body, [node_shape, f32(10, part_rows, L)], [pltpu.VMEM((10, r...  2.78 us

profile of v3, /device:TPU:0, one launch (start us, length us, event | category | flops | bytes accessed | tf_op | source)
XLA Modules:
  0.0 98.3 jit_solution(4651554116969723226)
XLA Ops:
  0.6 0.9 reduce-precision_convert_fusion
  1.6 0.1 pad.11.clone
  1.6 0.1 maximum_maximum_fusion
  1.7 0.1 convert_element_type.9
  1.9 0.5 copy-done.16
  2.4 0.2 convolution_convert_fusion
  2.7 0.2 reshape.63.refs_4_
  2.9 0.4 copy-done.15
  3.3 0.2 copy-done.6
  3.6 0.8 copy-done.7
  4.4 10.6 %elements.3 = (f32[3,32,128]{2,1,0:T(8,128)S(1)}, f32[5,8,128]{2,1,0:T(8,128)S(1)}) custom-call(f32[3,32,128]{2,1,0:T(8,128)S(1)} %get-tuple-element.50.refs_0_, f32[3,32,128]{2,1,0:T(8,128)S(1)} %get-tuple-element.49.refs_1_, s32[8,4096]{1,0:T(8,128)S(1)} %add_select_fusion.refs_2_, s32[8,128]{1,0:T(8,128)S(1)} %concatenate.13.refs_3_.shared_ref, ...), custom_call_target="tpu_custom_call" | custom-call | tf_op jit(solution)/shard_map/elements/pallas_call | solution.py:487
  15.1 7.4 %exchange.3.refs_6_ = f32[5,8,128]{2,1,0:T(8,128)S(1)} custom-call(f32[5,8,128]{2,1,0:T(8,128)S(1)} %get-tuple-element.23.own_ref), custom_call_target="tpu_custom_call" | custom-call | tf_op jit(solution)/shard_map/exchange/pallas_call | solution.py:423
  22.6 0.7 copy-done
  23.3 11.5 %elements.4 = (f32[3,32,128]{2,1,0:T(8,128)S(1)}, f32[5,8,128]{2,1,0:T(8,128)S(1)}, f32[3,32,128]{2,1,0:T(8,128)S(1)}, f32[3,32,128]{2,1,0:T(8,128)S(1)}) custom-call(f32[3,32,128]{2,1,0:T(8,128)S(1)} %get-tuple-element.50.refs_0_, f32[3,32,128]{2,1,0:T(8,128)S(1)} %get-tuple-element.49.refs_1_, s32[8,4096]{1,0:T(8,128)S(1)} %add_select_fusion.refs_2_, ...), custom_call_target="tpu_custom_call" | custom-call | tf_op jit(solution)/shard_map/elements/pallas_call | solution.py:491
  34.7 4.7 %exchange.4.refs_6_ = f32[5,8,128]{2,1,0:T(8,128)S(1)} custom-call(f32[5,8,128]{2,1,0:T(8,128)S(1)} %get-tuple-element.27.own_ref), custom_call_target="tpu_custom_call" | custom-call | tf_op jit(solution)/shard_map/exchange/pallas_call | solution.py:423
  39.5 11.5 %elements.5 = (f32[3,32,128]{2,1,0:T(8,128)S(1)}, f32[5,8,128]{2,1,0:T(8,128)S(1)}, f32[3,32,128]{2,1,0:T(8,128)S(1)}, f32[3,32,128]{2,1,0:T(8,128)S(1)}) custom-call(f32[3,32,128]{2,1,0:T(8,128)S(1)} %get-tuple-element.24.refs_0_, f32[3,32,128]{2,1,0:T(8,128)S(1)} %get-tuple-element.25.refs_1_, s32[8,4096]{1,0:T(8,128)S(1)} %add_select_fusion.refs_2_, ...), custom_call_target="tpu_custom_call" | custom-call | tf_op jit(solution)/shard_map/elements/pallas_call | solution.py:491
  50.9 4.7 %exchange.5.rec_ref = f32[5,8,128]{2,1,0:T(8,128)S(1)} custom-call(f32[5,8,128]{2,1,0:T(8,128)S(1)} %get-tuple-element.31.own_ref), custom_call_target="tpu_custom_call" | custom-call | tf_op jit(solution)/shard_map/exchange/pallas_call | solution.py:423
  55.7 0.7 copy-done.4
  56.4 1.2 %slots.1 = (s32[16,128]{1,0:T(8,128)S(1)}, f32[4,64,128]{2,1,0:T(8,128)S(1)}) custom-call(s32[16,128]{1,0:T(8,128)S(1)} %bitcast.57, s32[16,128]{1,0:T(8,128)S(1)} %bitcast.58, f32[3,16,128]{2,1,0:T(8,128)S(1)} %bitcast.44), custom_call_target="tpu_custom_call" | custom-call | tf_op jit(solution)/shard_map/slots/pallas_call | solution.py:476
  57.7 1.8 %project.1 = (f32[3,32,128]{2,1,0:T(8,128)S(1)}, f32[3,32,128]{2,1,0:T(8,128)S(1)}, f32[3,32,128]{2,1,0:T(8,128)S(1)}, f32[2,64,128]{2,1,0:T(8,128)S(1)}) custom-call(f32[3,32,128]{2,1,0:T(8,128)S(1)} %get-tuple-element.28.u_ref, f32[3,32,128]{2,1,0:T(8,128)S(1)} %get-tuple-element.29.v_ref, s32[8,128]{1,0:T(8,128)S(1)} %concatenate.13.refs_3_.shared_ref, ...), custom_call_target="tpu_custom_call" | custom-call | tf_op jit(solution)/shard_map/project/pallas_call | solution.py:498
  59.5 0.1 copy.23.in_ref
  59.7 8.5 %swap.2 = f32[32,12,128]{2,1,0:T(8,128)S(1)} custom-call(f32[32,12,128]{2,1,0:T(8,128)S(1)} %copy.23.in_ref), custom_call_target="tpu_custom_call" | custom-call | tf_op jit(solution)/shard_map/swap/pallas_call | solution.py:415
  68.1 0.1 copy.24
  68.2 0.2 copy.25
  68.4 4.2 %push.1 = (f32[64,128]{1,0:T(8,128)S(1)}, f32[3,32,128]{2,1,0:T(8,128)S(1)}) custom-call(f32[3,32,128]{2,1,0:T(8,128)S(1)} %get-tuple-element.33.x_ref, f32[3,32,128]{2,1,0:T(8,128)S(1)} %get-tuple-element.34.v_ref, f32[6,64,128]{2,1,0:T(8,128)S(1)} %bitcast.43), custom_call_target="tpu_custom_call" | custom-call | tf_op jit(solution)/shard_map/push/pallas_call | solution.py:505
  72.6 9.6 %swap.3 = f32[32,2,128]{2,1,0:T(2,128)S(1)} custom-call(f32[32,2,128]{2,1,0:T(2,128)S(1)} %bitcast.55), custom_call_target="tpu_custom_call" | custom-call | tf_op jit(solution)/shard_map/swap/pallas_call | solution.py:415
  82.2 2.8 %finish.1 = (f32[3,32,128]{2,1,0:T(8,128)S(1)}, f32[10,4,128]{2,1,0:T(4,128)S(1)}) custom-call(f32[3,32,128]{2,1,0:T(8,128)S(1)} %get-tuple-element.33.x_ref, f32[3,32,128]{2,1,0:T(8,128)S(1)} %get-tuple-element.34.v_ref, f32[3,32,128]{2,1,0:T(8,128)S(1)} %get-tuple-element.35.as_ref, f32[3,32,128]{2,1,0:T(8,128)S(1)} %get-tuple-element.52.refs_7_.ext_ref, ...), custom_call_target="tpu_custom_call" | custom-call | tf_op jit(solution)/shard_map/finish/pallas_call | solution.py:509
  85.0 10.5 %total.1 = f32[10,4,128]{2,1,0:T(4,128)S(1)} custom-call(f32[10,4,128]{2,1,0:T(4,128)S(1)} %get-tuple-element.41.in_ref), custom_call_target="tpu_custom_call" | custom-call | tf_op jit(solution)/shard_map/total/pallas_call | solution.py:431
  95.6 0.6 copy-done.12
  96.4 0.7 copy-done.14
  97.0 0.6 pad_maximum_fusion.1
  97.7 0.7 copy.41
  (42 shorter events, 0.3 us)
Async XLA Ops:
  1.7 0.7 copy-start.16
  2.6 0.7 copy-start.15
  2.6 0.9 copy-start.6
  3.5 0.8 copy-start.7
  3.6 0.9 copy-start.8
  4.4 18.1 %copy-start.9 = (f32[3,4096]{1,0:T(4,128)S(1)}, f32[3,4096]{1,0:T(4,128)}, u32[]{:S(2)}) copy-start(f32[3,4096]{1,0:T(4,128)} %param.18) | copy-start | bytes 147460
  4.4 18.1 %copy-start.10 = (f32[3,4096]{1,0:T(4,128)S(1)}, f32[3,4096]{1,0:T(4,128)}, u32[]{:S(2)}) copy-start(f32[3,4096]{1,0:T(4,128)} %param.21) | copy-start | bytes 147460
  22.5 0.7 copy-start
  22.6 0.7 copy-start.3
  50.9 4.8 %copy-start.11 = (f32[3,2048]{1,0:T(4,128)S(1)}, f32[3,2048]{1,0:T(4,128)}, u32[]{:S(2)}) copy-start(f32[3,2048]{1,0:T(4,128)} %param.31) | copy-start | bytes 73732
  55.7 0.7 copy-start.4
  55.7 0.7 copy-start.5
  56.4 1.2 %copy-start.1 = (s32[2048]{0:T(1024)S(1)}, s32[2048]{0:T(1024)}, u32[]{:S(2)}) copy-start(s32[2048]{0:T(1024)} %param.28) | copy-start | bytes 24580
  72.6 9.6 %copy-start.2 = (s32[4096]{0:T(1024)S(1)}, s32[4096]{0:T(1024)}, u32[]{:S(2)}) copy-start(s32[4096]{0:T(1024)} %param.32) | copy-start | bytes 49156
  95.6 0.7 copy-start.12
  95.6 0.7 copy-start.13
  96.3 0.7 copy-start.14

commit v4 on v3

--- a/solution.py
+++ b/solution.py
@@ -233,7 +233,7 @@
         total[...] += scatter_tile(master, [-push * normal[c] for c in range(3)], rows, 2)
         return carry
 
-    lax.fori_loop(0, push_ref.shape[0] // 8, step, 0)
+    lax.fori_loop(0, push_ref.shape[0] // 8, step, 0, unroll=4)
     for c, value in enumerate(unstack(total[...], 3, rows, 2)):
         force_ref[c] = value
 
@@ -270,7 +270,7 @@
         total[...] += scatter_tile(part, [vals[k, sl, :] for k in range(10)], part_rows, 3)
         return carry
 
-    lax.fori_loop(0, rows // 8, step, 0)
+    lax.fori_loop(0, rows // 8, step, 0, unroll=2)
     for k, value in enumerate(unstack(total[...], 10, part_rows, 3)):
         sums_ref[k] = value
 

time: 98.9 us -> 96.8 us (0.979)
  Pallas kernels: 89.1 us -> 87.1 us
    pallas_call x1, Pallas kernels: 4.21 us -> 2.55 us  [per_device(): call(push_body, [f32(slot_rows, L), node_shape], [pltpu.VMEM((6 * rows, L...]
where the time goes in v4:
time: 96.8 us; the launch traced here: 96.3 us
  Pallas kernels  87.1 us (90%)
  local copies, waits for them, and re-layouts  6.25 us (6%)
  other arithmetic  1.75 us (2%)
  between operations  1 us (1%)
    pallas_call x2, Pallas kernels, per_device(): call(functools.partial(elem_body, False, neighbours), [node_shape, own_sh...  22.9 us
    pallas_call x2, Pallas kernels, swap(): call(functools.partial(swap_body, domains), [f32(*payload.shape)], [pltpu...  18.1 us
    pallas_call x3, Pallas kernels, exchange(): call(functools.partial(exchange_body, neighbours), [f32(*own.shape)], [pl...  16.9 us
    pallas_call x1, Pallas kernels, per_device(): call(functools.partial(elem_body, True, neighbours), [node_shape, own_sha...  10.6 us
    pallas_call x1, Pallas kernels, total_over(): call(functools.partial(total_body, domains), [f32(*sums.shape)], [pltpu.V...  10.5 us
    unnamed x39, local copies, waits for them, and re-layouts  5.43 us
    pallas_call x1, Pallas kernels, per_device(): call(push_body, [f32(slot_rows, L), node_shape], [pltpu.VMEM((6 * rows, L...  2.55 us
    pallas_call x1, Pallas kernels, per_device(): call(finish_body, [node_shape, f32(10, part_rows, L)], [pltpu.VMEM((10, r...  2.44 us

profile of v4, /device:TPU:0, one launch (start us, length us, event | category | flops | bytes accessed | tf_op | source)
XLA Modules:
  0.0 96.3 jit_solution(3592226790236491351)
XLA Ops:
  0.6 0.9 reduce-precision_convert_fusion
  1.6 0.1 pad.11.clone
  1.6 0.1 maximum_maximum_fusion
  1.7 0.1 convert_element_type.9
  1.9 0.5 copy-done.16
  2.4 0.2 convolution_convert_fusion
  2.7 0.2 reshape.63.refs_4_
  2.9 0.4 copy-done.15
  3.3 0.2 copy-done.6
  3.6 0.8 copy-done.7
  4.4 10.6 %elements.3 = (f32[3,32,128]{2,1,0:T(8,128)S(1)}, f32[5,8,128]{2,1,0:T(8,128)S(1)}) custom-call(f32[3,32,128]{2,1,0:T(8,128)S(1)} %get-tuple-element.50.refs_0_, f32[3,32,128]{2,1,0:T(8,128)S(1)} %get-tuple-element.49.refs_1_, s32[8,4096]{1,0:T(8,128)S(1)} %add_select_fusion.refs_2_, s32[8,128]{1,0:T(8,128)S(1)} %concatenate.13.refs_3_.shared_ref, ...), custom_call_target="tpu_custom_call" | custom-call | tf_op jit(solution)/shard_map/elements/pallas_call | solution.py:487
  15.1 7.4 %exchange.3.refs_6_ = f32[5,8,128]{2,1,0:T(8,128)S(1)} custom-call(f32[5,8,128]{2,1,0:T(8,128)S(1)} %get-tuple-element.23.own_ref), custom_call_target="tpu_custom_call" | custom-call | tf_op jit(solution)/shard_map/exchange/pallas_call | solution.py:423
  22.6 0.7 copy-done
  23.3 11.5 %elements.4 = (f32[3,32,128]{2,1,0:T(8,128)S(1)}, f32[5,8,128]{2,1,0:T(8,128)S(1)}, f32[3,32,128]{2,1,0:T(8,128)S(1)}, f32[3,32,128]{2,1,0:T(8,128)S(1)}) custom-call(f32[3,32,128]{2,1,0:T(8,128)S(1)} %get-tuple-element.50.refs_0_, f32[3,32,128]{2,1,0:T(8,128)S(1)} %get-tuple-element.49.refs_1_, s32[8,4096]{1,0:T(8,128)S(1)} %add_select_fusion.refs_2_, ...), custom_call_target="tpu_custom_call" | custom-call | tf_op jit(solution)/shard_map/elements/pallas_call | solution.py:491
  34.7 4.7 %exchange.4.refs_6_ = f32[5,8,128]{2,1,0:T(8,128)S(1)} custom-call(f32[5,8,128]{2,1,0:T(8,128)S(1)} %get-tuple-element.27.own_ref), custom_call_target="tpu_custom_call" | custom-call | tf_op jit(solution)/shard_map/exchange/pallas_call | solution.py:423
  39.5 11.5 %elements.5 = (f32[3,32,128]{2,1,0:T(8,128)S(1)}, f32[5,8,128]{2,1,0:T(8,128)S(1)}, f32[3,32,128]{2,1,0:T(8,128)S(1)}, f32[3,32,128]{2,1,0:T(8,128)S(1)}) custom-call(f32[3,32,128]{2,1,0:T(8,128)S(1)} %get-tuple-element.24.refs_0_, f32[3,32,128]{2,1,0:T(8,128)S(1)} %get-tuple-element.25.refs_1_, s32[8,4096]{1,0:T(8,128)S(1)} %add_select_fusion.refs_2_, ...), custom_call_target="tpu_custom_call" | custom-call | tf_op jit(solution)/shard_map/elements/pallas_call | solution.py:491
  50.9 4.7 %exchange.5.rec_ref = f32[5,8,128]{2,1,0:T(8,128)S(1)} custom-call(f32[5,8,128]{2,1,0:T(8,128)S(1)} %get-tuple-element.31.own_ref), custom_call_target="tpu_custom_call" | custom-call | tf_op jit(solution)/shard_map/exchange/pallas_call | solution.py:423
  55.7 0.7 copy-done.4
  56.4 1.2 %slots.1 = (s32[16,128]{1,0:T(8,128)S(1)}, f32[4,64,128]{2,1,0:T(8,128)S(1)}) custom-call(s32[16,128]{1,0:T(8,128)S(1)} %bitcast.57, s32[16,128]{1,0:T(8,128)S(1)} %bitcast.58, f32[3,16,128]{2,1,0:T(8,128)S(1)} %bitcast.44), custom_call_target="tpu_custom_call" | custom-call | tf_op jit(solution)/shard_map/slots/pallas_call | solution.py:476
  57.7 1.8 %project.1 = (f32[3,32,128]{2,1,0:T(8,128)S(1)}, f32[3,32,128]{2,1,0:T(8,128)S(1)}, f32[3,32,128]{2,1,0:T(8,128)S(1)}, f32[2,64,128]{2,1,0:T(8,128)S(1)}) custom-call(f32[3,32,128]{2,1,0:T(8,128)S(1)} %get-tuple-element.28.u_ref, f32[3,32,128]{2,1,0:T(8,128)S(1)} %get-tuple-element.29.v_ref, s32[8,128]{1,0:T(8,128)S(1)} %concatenate.13.refs_3_.shared_ref, ...), custom_call_target="tpu_custom_call" | custom-call | tf_op jit(solution)/shard_map/project/pallas_call | solution.py:498
  59.5 0.1 copy.23.in_ref
  59.7 8.5 %swap.2 = f32[32,12,128]{2,1,0:T(8,128)S(1)} custom-call(f32[32,12,128]{2,1,0:T(8,128)S(1)} %copy.23.in_ref), custom_call_target="tpu_custom_call" | custom-call | tf_op jit(solution)/shard_map/swap/pallas_call | solution.py:415
  68.1 0.1 copy.24
  68.2 0.2 copy.25
  68.4 2.6 %push.1 = (f32[64,128]{1,0:T(8,128)S(1)}, f32[3,32,128]{2,1,0:T(8,128)S(1)}) custom-call(f32[3,32,128]{2,1,0:T(8,128)S(1)} %get-tuple-element.33.x_ref, f32[3,32,128]{2,1,0:T(8,128)S(1)} %get-tuple-element.34.v_ref, f32[6,64,128]{2,1,0:T(8,128)S(1)} %bitcast.43), custom_call_target="tpu_custom_call" | custom-call | tf_op jit(solution)/shard_map/push/pallas_call | solution.py:505
  70.9 9.6 %swap.3 = f32[32,2,128]{2,1,0:T(2,128)S(1)} custom-call(f32[32,2,128]{2,1,0:T(2,128)S(1)} %bitcast.55), custom_call_target="tpu_custom_call" | custom-call | tf_op jit(solution)/shard_map/swap/pallas_call | solution.py:415
  80.6 2.4 %finish.1 = (f32[3,32,128]{2,1,0:T(8,128)S(1)}, f32[10,4,128]{2,1,0:T(4,128)S(1)}) custom-call(f32[3,32,128]{2,1,0:T(8,128)S(1)} %get-tuple-element.33.x_ref, f32[3,32,128]{2,1,0:T(8,128)S(1)} %get-tuple-element.34.v_ref, f32[3,32,128]{2,1,0:T(8,128)S(1)} %get-tuple-element.35.as_ref, f32[3,32,128]{2,1,0:T(8,128)S(1)} %get-tuple-element.52.refs_7_.ext_ref, ...), custom_call_target="tpu_custom_call" | custom-call | tf_op jit(solution)/shard_map/finish/pallas_call | solution.py:509
  83.0 10.5 %total.1 = f32[10,4,128]{2,1,0:T(4,128)S(1)} custom-call(f32[10,4,128]{2,1,0:T(4,128)S(1)} %get-tuple-element.41.in_ref), custom_call_target="tpu_custom_call" | custom-call | tf_op jit(solution)/shard_map/total/pallas_call | solution.py:431
  93.6 0.6 copy-done.12
  94.3 0.7 copy-done.14
  95.0 0.6 pad_maximum_fusion.1
  95.6 0.7 copy.41
  (42 shorter events, 0.3 us)
Async XLA Ops:
  1.7 0.7 copy-start.16
  2.6 0.7 copy-start.15
  2.6 0.9 copy-start.6
  3.5 0.8 copy-start.7
  3.6 0.9 copy-start.8
  4.4 18.1 %copy-start.9 = (f32[3,4096]{1,0:T(4,128)S(1)}, f32[3,4096]{1,0:T(4,128)}, u32[]{:S(2)}) copy-start(f32[3,4096]{1,0:T(4,128)} %param.18) | copy-start | bytes 147460
  4.4 18.1 %copy-start.10 = (f32[3,4096]{1,0:T(4,128)S(1)}, f32[3,4096]{1,0:T(4,128)}, u32[]{:S(2)}) copy-start(f32[3,4096]{1,0:T(4,128)} %param.21) | copy-start | bytes 147460
  22.5 0.7 copy-start
  22.6 0.7 copy-start.3
  50.9 4.8 %copy-start.11 = (f32[3,2048]{1,0:T(4,128)S(1)}, f32[3,2048]{1,0:T(4,128)}, u32[]{:S(2)}) copy-start(f32[3,2048]{1,0:T(4,128)} %param.31) | copy-start | bytes 73732
  55.7 0.7 copy-start.4
  55.7 0.7 copy-start.5
  56.4 1.2 %copy-start.1 = (s32[2048]{0:T(1024)S(1)}, s32[2048]{0:T(1024)}, u32[]{:S(2)}) copy-start(s32[2048]{0:T(1024)} %param.28) | copy-start | bytes 24580
  70.9 9.6 %copy-start.2 = (s32[4096]{0:T(1024)S(1)}, s32[4096]{0:T(1024)}, u32[]{:S(2)}) copy-start(s32[4096]{0:T(1024)} %param.32) | copy-start | bytes 49156
  93.6 0.7 copy-start.12
  93.6 0.7 copy-start.13
  94.3 0.7 copy-start.14
